TPU v7x, 32 devices: a whole 2x2x4 slice. The times are simulated.
32 devices in a mesh: graph: 8 (over z, x), batch: 4 (over y, core).
Axes of the slice: x: 2, y: 2, z: 4, core: 2. Of those that a mesh axis runs over, the one named last changes fastest.
Arguments:
- layer_input: bfloat16 [2048, 512], P('graph', 'batch'), may hold values from -6 to 6
- hidden_state: bfloat16 [2048, 512], P('graph', 'batch'), may hold values from -6 to 6
- hidden_grad: bfloat16 [2048, 512], P('graph', 'batch'), may hold values from -6 to 6
- gate_weight: bfloat16 [640, 128], replicated, may hold values from -0.25 to 0.25
- gate_bias: float32 [128], replicated, may hold values from -3 to 3
- candidate_weight: bfloat16 [640, 64], replicated, may hold values from -0.25 to 0.25
- candidate_bias: float32 [64], replicated, may hold values from -3 to 3
- forward_tiles: bfloat16 [16, 3, 128, 128], P('graph'), as said below
- forward_columns: int32 [16, 3], P('graph'), may hold values from 0 to 2
- reverse_tiles: bfloat16 [16, 3, 128, 128], P('graph'), as said below
- reverse_columns: int32 [16, 3], P('graph'), may hold values from 0 to 2
- send_rows: int32 [8, 4, 32], P('graph'), may hold values from 0 to 255
- send_count: int32 [8, 4], P('graph'), may hold values from 1 to 32, as said below
Outputs:
- input_grad: float32 [2048, 512], P('graph', 'batch')
- state_grad: float32 [2048, 512], P('graph', 'batch')
- gate_weight_grad: float32 [640, 128], replicated
- gate_bias_grad: float32 [128], replicated
- candidate_weight_grad: float32 [640, 64], replicated
- candidate_bias_grad: float32 [64], replicated
Inputs may be any that keep to these rules, and one draw needn't show every extreme that they name: send_rows[p, j] lists rows of part p that part p + o_j reads; a row may stand in several lists or twice in one. The first send_count[p, j] entries of send_rows[p, j] are live; 32 is reached in every draw. `forward_tiles`: entries are zero or positive. `reverse_tiles`: entries are zero or positive. `forward_columns`: a value below 2 names a block of the part's own rows, a larger one a block of its rim. `reverse_columns`: as for forward_columns.
All inputs are finite; a program needn't handle non-finite values.
Results may differ from a plain program's by a relative error of at most 0.0055.
Values may be sent and summed in bfloat16 or wider, within the bound.
A program may use at most 64 MiB of HBM per device.

v0:
```python
import math

import jax
import jax.numpy as jnp
from jax import lax
from jax.sharding import PartitionSpec as P

HID = 64
INP = 64
KS = 5
CH = 128


def passed_along(value, axis, steps):
    count = lax.axis_size(axis)
    initial, last = (max(0, -steps), min(count, count - steps))
    return lax.ppermute(value, axis, [(source, source + steps) for source in range(initial, last)])


def rim_offsets(set_count):
    return [(number // 2 + 1) * (1 - 2 * (number % 2)) for number in range(set_count)]


def outgoing(values, send_rows, send_count):
    slot_ids = jnp.arange(send_rows.shape[2], dtype=jnp.int32)
    parcels = [values]
    for number, offset in enumerate(rim_offsets(send_rows.shape[1])):
        keep_mask = (slot_ids < send_count[0, number])[:, None]
        parcel = jnp.where(
            keep_mask, jnp.take(values, send_rows[0, number], axis=0), jnp.zeros((), values.dtype)
        )
        parcels.append(passed_along(parcel, "graph", offset))
    return jnp.concatenate(parcels, 0)


def incoming(rim_rows, send_rows, send_count, node_count):
    slot_count = send_rows.shape[2]
    slot_ids = jnp.arange(slot_count, dtype=jnp.int32)
    arrivals = []
    for number, offset in enumerate(rim_offsets(send_rows.shape[1])):
        parcel = rim_rows[number * slot_count : (number + 1) * slot_count]
        arrived = passed_along(parcel.astype(jnp.bfloat16), "graph", -offset).astype(parcel.dtype)
        keep_mask = (slot_ids < send_count[0, number])[:, None]
        arrivals.append(jnp.where(keep_mask, arrived, jnp.zeros((), arrived.dtype)))
    summed = jnp.zeros((node_count, rim_rows.shape[1]), jnp.float32)
    return summed.at[send_rows[0].reshape(-1)].add(jnp.concatenate(arrivals, 0))


def spread(extended, tiles, columns):
    tile_rows = tiles.shape[2]
    blocks = extended.reshape(extended.shape[0] // tile_rows, tile_rows, extended.shape[1])
    picked = jnp.take(blocks, columns, axis=0)
    result = jnp.einsum("itac,itcm->iam", tiles, picked, preferred_element_type=jnp.float32)
    return result.reshape(-1, extended.shape[1])


def gather_back(cotangents, tiles, columns, block_total):
    row_count = tiles.shape[0]
    tile_rows = tiles.shape[2]
    row_blocks = cotangents.reshape(row_count, tile_rows, -1)
    products = jnp.einsum("itac,iam->itcm", tiles, row_blocks, preferred_element_type=jnp.float32)
    select = (
        columns[:, :, None] == jnp.arange(block_total, dtype=jnp.int32)[None, None, :]
    ).astype(jnp.float32)
    blocks = jnp.einsum("itb,itcm->bcm", select, products, precision=lax.Precision.HIGHEST)
    blocks = blocks.reshape(block_total * tile_rows, -1)
    local_rows = row_count * tile_rows
    return (blocks[:local_rows], blocks[local_rows:])


def supports(values, links):
    forward_tiles, forward_columns, reverse_tiles, reverse_columns, send_rows, send_count = links
    feature_width = values.shape[1]
    extended = outgoing(values, send_rows, send_count)
    first_forward = spread(extended, forward_tiles, forward_columns).astype(jnp.bfloat16)
    first_reverse = spread(extended, reverse_tiles, reverse_columns).astype(jnp.bfloat16)
    stacked = outgoing(jnp.concatenate([first_forward, first_reverse], 1), send_rows, send_count)
    base_field = values.astype(jnp.float32)
    second_forward = (
        2.0 * spread(stacked[:, :feature_width], forward_tiles, forward_columns) - base_field
    ).astype(jnp.bfloat16)
    second_reverse = (
        2.0 * spread(stacked[:, feature_width:], reverse_tiles, reverse_columns) - base_field
    ).astype(jnp.bfloat16)
    return [values, first_forward, second_forward, first_reverse, second_reverse]


def back_supports(flat_grads, node_count, samples, links):
    forward_tiles, forward_columns, reverse_tiles, reverse_columns, send_rows, send_count = links
    tile_rows = forward_tiles.shape[2]
    block_total = (node_count + send_rows.shape[1] * send_rows.shape[2]) // tile_rows
    feature_width = samples * CH
    per_node = flat_grads.reshape(node_count, samples, KS, CH)
    members = [per_node[:, :, support].reshape(node_count, feature_width) for support in range(KS)]
    local_forward, rim_forward = gather_back(
        members[2].astype(jnp.bfloat16), forward_tiles, forward_columns, block_total
    )
    local_reverse, rim_reverse = gather_back(
        members[4].astype(jnp.bfloat16), reverse_tiles, reverse_columns, block_total
    )
    returned = incoming(
        jnp.concatenate([rim_forward, rim_reverse], 1), send_rows, send_count, node_count
    )
    first_forward = members[1] + 2.0 * (local_forward + returned[:, :feature_width])
    first_reverse = members[3] + 2.0 * (local_reverse + returned[:, feature_width:])
    local_forward, rim_forward = gather_back(
        first_forward.astype(jnp.bfloat16), forward_tiles, forward_columns, block_total
    )
    local_reverse, rim_reverse = gather_back(
        first_reverse.astype(jnp.bfloat16), reverse_tiles, reverse_columns, block_total
    )
    summed = (
        local_forward
        + local_reverse
        + incoming(rim_forward + rim_reverse, send_rows, send_count, node_count)
    )
    summed = members[0] - members[2] - members[4] + summed
    return summed.reshape(-1, CH)


def on_device(
    layer_input,
    hidden_state,
    hidden_grad,
    gate_weight,
    gate_bias,
    candidate_weight,
    candidate_bias,
    forward_tiles,
    forward_columns,
    reverse_tiles,
    reverse_columns,
    send_rows,
    send_count,
):
    node_count = layer_input.shape[0]
    samples = layer_input.shape[1] // INP
    links = (forward_tiles, forward_columns, reverse_tiles, reverse_columns, send_rows, send_count)
    input_field = layer_input.reshape(node_count, samples, INP)
    hidden_field = hidden_state.reshape(node_count, samples, HID)
    stacked = jnp.concatenate([input_field, hidden_field], 2).reshape(node_count, samples * CH)
    gate_support = supports(stacked, links)
    gate_rows = jnp.concatenate([member.reshape(-1, CH) for member in gate_support], 1)
    gate_values = jax.nn.sigmoid(
        jnp.dot(gate_rows, gate_weight, preferred_element_type=jnp.float32) + gate_bias
    )
    reset_gate = gate_values[:, :HID]
    update = gate_values[:, HID:]
    hidden_rows = hidden_state.reshape(-1, HID).astype(jnp.float32)
    gated = (reset_gate * hidden_rows).astype(jnp.bfloat16)
    candidate_input = jnp.concatenate(
        [input_field, gated.reshape(node_count, samples, HID)], 2
    ).reshape(node_count, samples * CH)
    candidate_rows = jnp.concatenate(
        [member.reshape(-1, CH) for member in supports(candidate_input, links)], 1
    )
    candidate = jnp.tanh(
        jnp.dot(candidate_rows, candidate_weight, preferred_element_type=jnp.float32)
        + candidate_bias
    )
    cotangent = hidden_grad.reshape(-1, HID).astype(jnp.float32)
    update_grad = cotangent * (hidden_rows - candidate)
    candidate_grad = (cotangent * (1.0 - update) * (1.0 - candidate * candidate)).astype(
        jnp.bfloat16
    )
    candidate_sums = jnp.dot(candidate_rows.T, candidate_grad, preferred_element_type=jnp.float32)
    candidate_totals = jnp.sum(candidate_grad.astype(jnp.float32), 0)
    mixed_grad = back_supports(
        jnp.dot(candidate_grad, candidate_weight.T, preferred_element_type=jnp.float32),
        node_count,
        samples,
        links,
    )
    gated_grad = mixed_grad[:, INP:]
    reset_grad = gated_grad * hidden_rows
    gate_grad = jnp.concatenate(
        [reset_grad * reset_gate * (1.0 - reset_gate), update_grad * update * (1.0 - update)], 1
    ).astype(jnp.bfloat16)
    gate_sums = jnp.dot(gate_rows.T, gate_grad, preferred_element_type=jnp.float32)
    gate_totals = jnp.sum(gate_grad.astype(jnp.float32), 0)
    stacked_grad = back_supports(
        jnp.dot(gate_grad, gate_weight.T, preferred_element_type=jnp.float32),
        node_count,
        samples,
        links,
    )
    input_total = mixed_grad[:, :INP] + stacked_grad[:, :INP]
    hidden_total = cotangent * update + gated_grad * reset_gate + stacked_grad[:, INP:]
    gate_sums, gate_totals, candidate_sums, candidate_totals = lax.psum(
        (gate_sums, gate_totals, candidate_sums, candidate_totals), ("graph", "batch")
    )
    norm_scale = 1.0 / math.sqrt(
        node_count * lax.axis_size("graph") * samples * lax.axis_size("batch")
    )
    return (
        input_total.reshape(node_count, samples * INP),
        hidden_total.reshape(node_count, samples * HID),
        gate_sums * norm_scale,
        gate_totals * norm_scale,
        candidate_sums * norm_scale,
        candidate_totals * norm_scale,
    )


def solution(mesh):
    placed = (
        P("graph", "batch"),
        P("graph", "batch"),
        P("graph", "batch"),
        P(),
        P(),
        P(),
        P(),
        P("graph", None, None, None),
        P("graph", None),
        P("graph", None, None, None),
        P("graph", None),
        P("graph", None, None),
        P("graph", None),
    )
    return jax.shard_map(
        on_device,
        mesh=mesh,
        in_specs=placed,
        out_specs=(P("graph", "batch"), P("graph", "batch"), P(), P(), P(), P()),
        check_vma=False,
    )
```

profile of v0, /device:TPU:0, one launch (start us, length us, event | category | flops | bytes accessed | tf_op | source)
XLA Modules:
  0.0 376.2 jit_solution(6465244702838748584)
XLA Ops:
  7.2 1.4 fusion.138
  8.6 1.5 compare_and_fusion.2
  12.9 4.9 %collective-permute-start = (bf16[32,256]{1,0:T(8,128)(2,1)S(1)}, bf16[32,256]{1,0:T(8,128)(2,1)S(1)}, u32[]{:S(2)}, u32[]{:S(2)}) collective-permute-start(bf16[32,256]{1,0:T(8,128)(2,1)S(1)} %select_select_fusion.15), channel_id=1, source_target_pairs={{0,4},{4,8},{8,12},{12,16},{16,20},{20,24},{24,28},{1,5},{5,9},{9,... | collective-permute-start | bytes 49160 | tf_op jit(solution)/shard_map/ppermute | solution.py:17
  19.2 1.3 collective-permute-start.1
  21.9 5.5 %collective-permute-start.2 = (bf16[32,256]{1,0:T(8,128)(2,1)S(1)}, bf16[32,256]{1,0:T(8,128)(2,1)S(1)}, u32[]{:S(2)}, u32[]{:S(2)}) collective-permute-start(bf16[32,256]{1,0:T(8,128)(2,1)S(1)} %select_select_fusion.13), channel_id=1, source_target_pairs={{0,8},{4,12},{8,16},{12,20},{16,24},{20,28},{1,9},{5,13},{9,17},{1... | collective-permute-start | bytes 49160 | tf_op jit(solution)/shard_map/ppermute | solution.py:17
  28.8 1.3 collective-permute-start.3
  40.8 2.5 collective-permute-start.4
  43.5 1.3 collective-permute-start.7
  44.8 1.3 collective-permute-start.5
  46.1 7.5 %collective-permute-start.6 = (bf16[32,512]{1,0:T(8,128)(2,1)S(1)}, bf16[32,512]{1,0:T(8,128)(2,1)S(1)}, u32[]{:S(2)}, u32[]{:S(2)}) collective-permute-start(bf16[32,512]{1,0:T(8,128)(2,1)S(1)} %select_select_fusion.5), channel_id=1, source_target_pairs={{0,8},{4,12},{8,16},{12,20},{16,24},{20,28},{1,9},{5,13},{9,17},{1... | collective-permute-start | bytes 98312 | tf_op jit(solution)/shard_map/ppermute | solution.py:17
  53.6 1.5 collective-permute-done.6
  63.7 3.1 collective-permute-start.8
  66.8 1.3 collective-permute-start.9
  68.1 6.9 %collective-permute-start.10 = (bf16[32,256]{1,0:T(8,128)(2,1)S(1)}, bf16[32,256]{1,0:T(8,128)(2,1)S(1)}, u32[]{:S(2)}, u32[]{:S(2)}) collective-permute-start(bf16[32,256]{1,0:T(8,128)(2,1)S(1)} %select_select_fusion.9), channel_id=1, source_target_pairs={{0,8},{4,12},{8,16},{12,20},{16,24},{20,28},{1,9},{5,13},{9,17},{1... | collective-permute-start | bytes 49160 | tf_op jit(solution)/shard_map/ppermute | solution.py:17
  75.0 1.3 collective-permute-start.11
  76.4 4.5 %collective-permute-done.11 = bf16[32,256]{1,0:T(8,128)(2,1)S(1)} collective-permute-done((bf16[32,256]{1,0:T(8,128)(2,1)S(1)}, bf16[32,256]{1,0:T(8,128)(2,1)S(1)}, u32[]{:S(2)}, u32[]{:S(2)}) %collective-permute-start.11) | collective-permute-done | bytes 16416 | tf_op jit(solution)/shard_map/ppermute | solution.py:17
  86.5 2.5 collective-permute-start.12
  89.1 1.3 collective-permute-start.15
  90.4 1.3 collective-permute-start.13
  91.7 7.1 %collective-permute-start.14 = (bf16[32,512]{1,0:T(8,128)(2,1)S(1)}, bf16[32,512]{1,0:T(8,128)(2,1)S(1)}, u32[]{:S(2)}, u32[]{:S(2)}) collective-permute-start(bf16[32,512]{1,0:T(8,128)(2,1)S(1)} %select_select_fusion.1), channel_id=1, source_target_pairs={{0,8},{4,12},{8,16},{12,20},{16,24},{20,28},{1,9},{5,13},{9,17},{1... | collective-permute-start | bytes 98312 | tf_op jit(solution)/shard_map/ppermute | solution.py:17
  98.9 1.4 collective-permute-done.14
  104.7 1.5 convert_reduce_fusion.5
  106.9 1.5 fusion.139
  108.4 1.4 reshape.283
  109.8 2.4 convert_reduce_fusion.4
  112.2 3.5 slice_reduce_fusion.3
  118.4 1.7 convolution_bitcast_fusion.14
  121.8 1.7 convolution_bitcast_fusion.15
  123.8 1.4 collective-permute-start.16
  126.4 5.2 %collective-permute-start.19 = (bf16[32,512]{1,0:T(8,128)(2,1)S(1)}, bf16[32,512]{1,0:T(8,128)(2,1)S(1)}, u32[]{:S(2)}, u32[]{:S(2)}) collective-permute-start(bf16[32,512]{1,0:T(8,128)(2,1)S(1)} %get-tuple-element.65), channel_id=1, source_target_pairs={{0,8},{4,12},{8,16},{12,20},{16,24},{20,28},{1,9},{5,13},{9,17},{1... | collective-permute-start | bytes 98312 | tf_op jit(solution)/shard_map/ppermute | solution.py:17
  131.6 1.3 collective-permute-start.18
  132.9 4.1 %collective-permute-start.17 = (bf16[32,512]{1,0:T(8,128)(2,1)S(1)}, bf16[32,512]{1,0:T(8,128)(2,1)S(1)}, u32[]{:S(2)}, u32[]{:S(2)}) collective-permute-start(bf16[32,512]{1,0:T(8,128)(2,1)S(1)} %get-tuple-element.67), channel_id=1, source_target_pairs={{0,4},{4,8},{8,12},{12,16},{16,20},{20,24},{24,28},{1,5},{5,9},{9,... | collective-permute-start | bytes 98312 | tf_op jit(solution)/shard_map/ppermute | solution.py:17
  138.5 1.6 scatter_custom_fusion
  144.6 4.3 %collective-permute-start.21 = (bf16[32,256]{1,0:T(8,128)(2,1)S(1)}, bf16[32,256]{1,0:T(8,128)(2,1)S(1)}, u32[]{:S(2)}, u32[]{:S(2)}) collective-permute-start(bf16[32,256]{1,0:T(8,128)(2,1)S(1)} %bitcast.359), channel_id=1, source_target_pairs={{0,4},{4,8},{8,12},{12,16},{16,20},{20,24},{24,28},{1,5},{5,9},{9,... | collective-permute-start | bytes 49160 | tf_op jit(solution)/shard_map/ppermute | solution.py:17
  148.9 1.3 collective-permute-start.22
  150.2 5.4 %collective-permute-start.23 = (bf16[32,256]{1,0:T(8,128)(2,1)S(1)}, bf16[32,256]{1,0:T(8,128)(2,1)S(1)}, u32[]{:S(2)}, u32[]{:S(2)}) collective-permute-start(bf16[32,256]{1,0:T(8,128)(2,1)S(1)} %bitcast.356), channel_id=1, source_target_pairs={{0,8},{4,12},{8,16},{12,20},{16,24},{20,28},{1,9},{5,13},{9,17},{1... | collective-permute-start | bytes 49160 | tf_op jit(solution)/shard_map/ppermute | solution.py:17
  155.6 1.3 collective-permute-start.20
  157.2 4.4 %collective-permute-done.20 = bf16[32,256]{1,0:T(8,128)(2,1)S(1)} collective-permute-done((bf16[32,256]{1,0:T(8,128)(2,1)S(1)}, bf16[32,256]{1,0:T(8,128)(2,1)S(1)}, u32[]{:S(2)}, u32[]{:S(2)}) %collective-permute-start.20) | collective-permute-done | bytes 16416 | tf_op jit(solution)/shard_map/ppermute | solution.py:17
  161.7 1.5 scatter_custom_fusion.1
  165.3 1.5 fusion.108
  166.8 1.4 reshape.287
  168.2 1.7 convert_reduce_fusion.2
  169.9 3.6 slice_reduce_fusion.1
  173.5 42.8 %all-reduce = (f32[128]{0:T(128)S(1)}, f32[64]{0:T(128)}) all-reduce(f32[128]{0:T(128)} %convert_reduce_fusion, f32[64]{0:T(128)} %get-tuple-element.23), channel_id=1, replica_groups=mesh['graph'=8,'batch'=4] {'graph','batch'}, use_global_device_ids=true, to_apply=%region_6.10 | all-reduce | flops 192 | bytes 1536 | tf_op jit(solution)/shard_map/psum | solution.py:189
  218.4 1.7 convolution_bitcast_fusion.10
  221.8 1.7 convolution_bitcast_fusion.11
  224.6 1.3 collective-permute-start.24
  226.7 6.3 %collective-permute-start.27 = (bf16[32,512]{1,0:T(8,128)(2,1)S(1)}, bf16[32,512]{1,0:T(8,128)(2,1)S(1)}, u32[]{:S(2)}, u32[]{:S(2)}) collective-permute-start(bf16[32,512]{1,0:T(8,128)(2,1)S(1)} %get-tuple-element.57), channel_id=1, source_target_pairs={{0,8},{4,12},{8,16},{12,20},{16,24},{20,28},{1,9},{5,13},{9,17},{1... | collective-permute-start | bytes 98312 | tf_op jit(solution)/shard_map/ppermute | solution.py:17
  232.9 1.3 collective-permute-start.26
  234.2 1.3 collective-permute-start.25
  235.7 3.0 collective-permute-done.26
  238.9 1.6 scatter_custom_fusion.2
  240.5 1.7 fusion.38
  243.0 1.7 convolution_bitcast_fusion.8
  246.5 1.7 convolution_bitcast_fusion.9
  248.8 4.9 %collective-permute-start.29 = (bf16[32,256]{1,0:T(8,128)(2,1)S(1)}, bf16[32,256]{1,0:T(8,128)(2,1)S(1)}, u32[]{:S(2)}, u32[]{:S(2)}) collective-permute-start(bf16[32,256]{1,0:T(8,128)(2,1)S(1)} %bitcast.360), channel_id=1, source_target_pairs={{0,4},{4,8},{8,12},{12,16},{16,20},{20,24},{24,28},{1,5},{5,9},{9,... | collective-permute-start | bytes 49160 | tf_op jit(solution)/shard_map/ppermute | solution.py:17
  253.8 1.3 collective-permute-start.30
  255.1 4.5 %collective-permute-start.31 = (bf16[32,256]{1,0:T(8,128)(2,1)S(1)}, bf16[32,256]{1,0:T(8,128)(2,1)S(1)}, u32[]{:S(2)}, u32[]{:S(2)}) collective-permute-start(bf16[32,256]{1,0:T(8,128)(2,1)S(1)} %bitcast.355), channel_id=1, source_target_pairs={{0,8},{4,12},{8,16},{12,20},{16,24},{20,28},{1,9},{5,13},{9,17},{1... | collective-permute-start | bytes 49160 | tf_op jit(solution)/shard_map/ppermute | solution.py:17
  259.6 1.3 collective-permute-start.28
  261.2 5.2 %collective-permute-done.28 = bf16[32,256]{1,0:T(8,128)(2,1)S(1)} collective-permute-done((bf16[32,256]{1,0:T(8,128)(2,1)S(1)}, bf16[32,256]{1,0:T(8,128)(2,1)S(1)}, u32[]{:S(2)}, u32[]{:S(2)}) %collective-permute-start.28) | collective-permute-done | bytes 16416 | tf_op jit(solution)/shard_map/ppermute | solution.py:17
  266.5 1.5 scatter_custom_fusion.3
  270.1 95.6 %all-reduce.4.cloned.1.call-done = (f32[640,128]{1,0:T(8,128)}, f32[640,64]{0,1:T(8,128)}) async-done(((f32[640,128]{1,0:T(8,128)}, f32[640,64]{0,1:T(8,128)}), (f32[640,128]{1,0:T(8,128)}, f32[640,64]{0,1:T(8,128)})) %all-reduce.4.cloned.1.call-update) | async-done | bytes 491536 | tf_op jit(solution)/shard_map/psum | solution.py:189
  365.6 1.7 broadcast_multiply_fusion
  367.4 1.6 broadcast_multiply_fusion.1
  (345 shorter events, 61.3 us)
Async XLA Ops:
  7.2 30.0 %copy-start = (bf16[2,3,128,128]{3,2,1,0:T(8,128)(2,1)S(1)}, bf16[2,3,128,128]{3,2,1,0:T(8,128)(2,1)}, u32[]{:S(2)}) copy-start(bf16[2,3,128,128]{3,2,1,0:T(8,128)(2,1)} %param.28) | copy-start | bytes 589828
  7.2 28.3 %copy-start.17 = (bf16[256,128]{1,0:T(8,128)(2,1)S(1)}, bf16[256,128]{1,0:T(8,128)(2,1)}, u32[]{:S(2)}) copy-start(bf16[256,128]{1,0:T(8,128)(2,1)} %param.20) | copy-start | bytes 196612
  7.2 28.5 %copy-start.21 = (bf16[256,128]{1,0:T(8,128)(2,1)S(1)}, bf16[256,128]{1,0:T(8,128)(2,1)}, u32[]{:S(2)}) copy-start(bf16[256,128]{1,0:T(8,128)(2,1)} %param.21) | copy-start | bytes 196612
  7.2 358.4 %all-reduce.4.cloned.1.call-start = ((), (), s32[]{:S(2)}) async-start(), calls=%async_computation | async-start | bytes 983040 | tf_op jit(solution)/shard_map/psum | solution.py:189
  10.1 30.3 %copy-start.33 = (pred[32]{0:T(512)(128)(4,1)}, pred[32]{0:T(512)(128)(4,1)S(1)}, u32[]{:S(2)}) copy-start(pred[32]{0:T(512)(128)(4,1)S(1)} %get-tuple-element.68) | copy-start | bytes 100
  10.1 30.4 %copy-start.31 = (pred[32]{0:T(512)(128)(4,1)}, pred[32]{0:T(512)(128)(4,1)S(1)}, u32[]{:S(2)}) copy-start(pred[32]{0:T(512)(128)(4,1)S(1)} %get-tuple-element.70) | copy-start | bytes 100
  10.2 30.5 %copy-start.27 = (pred[32]{0:T(512)(128)(4,1)}, pred[32]{0:T(512)(128)(4,1)S(1)}, u32[]{:S(2)}) copy-start(pred[32]{0:T(512)(128)(4,1)S(1)} %get-tuple-element.72) | copy-start | bytes 100
  10.2 33.1 %copy-start.29 = (pred[32]{0:T(512)(128)(4,1)}, pred[32]{0:T(512)(128)(4,1)S(1)}, u32[]{:S(2)}) copy-start(pred[32]{0:T(512)(128)(4,1)S(1)} %get-tuple-element.27) | copy-start | bytes 100
  10.2 29.0 %copy-start.35 = (s32[1024]{0:T(1024)}, s32[1024]{0:T(1024)S(1)}, u32[]{:S(2)}) copy-start(s32[1024]{0:T(1024)S(1)} %pad_clamp_fusion.5) | copy-start | bytes 12292
  12.9 23.0 %collective-permute-start = (bf16[32,256]{1,0:T(8,128)(2,1)S(1)}, bf16[32,256]{1,0:T(8,128)(2,1)S(1)}, u32[]{:S(2)}, u32[]{:S(2)}) collective-permute-start(bf16[32,256]{1,0:T(8,128)(2,1)S(1)} %select_select_fusion.15), channel_id=1, source_target_pairs={{0,4},{4,8},{8,12},{12,16},{16,20},{20,24},{24,28},{1,5},{5,9},{9,... | collective-permute-start | bytes 49160 | tf_op jit(solution)/shard_map/ppermute | solution.py:17
  18.5 20.1 %copy-start.36 = (s32[1024]{0:T(1024)}, s32[1024]{0:T(1024)S(1)}, u32[]{:S(2)}) copy-start(s32[1024]{0:T(1024)S(1)} %pad_clamp_fusion.4) | copy-start | bytes 12292
  19.2 16.8 %collective-permute-start.1 = (bf16[32,256]{1,0:T(8,128)(2,1)S(1)}, bf16[32,256]{1,0:T(8,128)(2,1)S(1)}, u32[]{:S(2)}, u32[]{:S(2)}) collective-permute-start(bf16[32,256]{1,0:T(8,128)(2,1)S(1)} %select_select_fusion.14), channel_id=1, source_target_pairs={{4,0},{8,4},{12,8},{16,12},{20,16},{24,20},{28,24},{5,1},{9,5},{13... | collective-permute-start | bytes 49160 | tf_op jit(solution)/shard_map/ppermute | solution.py:17
  21.2 16.7 %copy-start.37 = (s32[1024]{0:T(1024)}, s32[1024]{0:T(1024)S(1)}, u32[]{:S(2)}) copy-start(s32[1024]{0:T(1024)S(1)} %pad_clamp_fusion.3) | copy-start | bytes 12292
  21.9 14.1 %collective-permute-start.2 = (bf16[32,256]{1,0:T(8,128)(2,1)S(1)}, bf16[32,256]{1,0:T(8,128)(2,1)S(1)}, u32[]{:S(2)}, u32[]{:S(2)}) collective-permute-start(bf16[32,256]{1,0:T(8,128)(2,1)S(1)} %select_select_fusion.13), channel_id=1, source_target_pairs={{0,8},{4,12},{8,16},{12,20},{16,24},{20,28},{1,9},{5,13},{9,17},{1... | collective-permute-start | bytes 49160 | tf_op jit(solution)/shard_map/ppermute | solution.py:17
  28.1 11.7 %copy-start.38 = (s32[1024]{0:T(1024)}, s32[1024]{0:T(1024)S(1)}, u32[]{:S(2)}) copy-start(s32[1024]{0:T(1024)S(1)} %pad_clamp_fusion.2) | copy-start | bytes 12292
  28.8 7.2 %collective-permute-start.3 = (bf16[32,256]{1,0:T(8,128)(2,1)S(1)}, bf16[32,256]{1,0:T(8,128)(2,1)S(1)}, u32[]{:S(2)}, u32[]{:S(2)}) collective-permute-start(bf16[32,256]{1,0:T(8,128)(2,1)S(1)} %select_select_fusion.12), channel_id=1, source_target_pairs={{8,0},{12,4},{16,8},{20,12},{24,16},{28,20},{9,1},{13,5},{17,9},{2... | collective-permute-start | bytes 49160 | tf_op jit(solution)/shard_map/ppermute | solution.py:17
  31.6 6.0 %copy-start.44 = (pred[2,3]{1,0:T(4,128)(4,1)}, pred[2,3]{1,0:T(4,128)(4,1)S(1)}, u32[]{:S(2)}) copy-start(pred[2,3]{1,0:T(4,128)(4,1)S(1)} %compare_and_fusion.1) | copy-start | bytes 22
  32.9 4.6 %copy-start.41 = (pred[2,3]{1,0:T(4,128)(4,1)}, pred[2,3]{1,0:T(4,128)(4,1)S(1)}, u32[]{:S(2)}) copy-start(pred[2,3]{1,0:T(4,128)(4,1)S(1)} %compare_and_fusion) | copy-start | bytes 22
  35.5 19.7 %copy-start.25 = (s32[1024]{0:T(1024)}, s32[1024]{0:T(1024)S(1)}, u32[]{:S(2)}) copy-start(s32[1024]{0:T(1024)S(1)} %get-tuple-element.79) | copy-start | bytes 12292
  35.7 69.0 %copy-start.11 = (bf16[512,64]{0,1:T(8,128)(2,1)}, bf16[512,64]{0,1:T(8,128)(2,1)S(1)}, u32[]{:S(2)}) copy-start(bf16[512,64]{0,1:T(8,128)(2,1)S(1)} %copy.406) | copy-start | bytes 196612
  40.8 12.8 %collective-permute-start.4 = (bf16[32,512]{1,0:T(8,128)(2,1)S(1)}, bf16[32,512]{1,0:T(8,128)(2,1)S(1)}, u32[]{:S(2)}, u32[]{:S(2)}) collective-permute-start(bf16[32,512]{1,0:T(8,128)(2,1)S(1)} %select_select_fusion.7), channel_id=1, source_target_pairs={{0,4},{4,8},{8,12},{12,16},{16,20},{20,24},{24,28},{1,5},{5,9},{9,... | collective-permute-start | bytes 98312 | tf_op jit(solution)/shard_map/ppermute | solution.py:17
  43.5 11.7 %collective-permute-start.7 = (bf16[32,512]{1,0:T(8,128)(2,1)S(1)}, bf16[32,512]{1,0:T(8,128)(2,1)S(1)}, u32[]{:S(2)}, u32[]{:S(2)}) collective-permute-start(bf16[32,512]{1,0:T(8,128)(2,1)S(1)} %select_select_fusion.4), channel_id=1, source_target_pairs={{8,0},{12,4},{16,8},{20,12},{24,16},{28,20},{9,1},{13,5},{17,9},{2... | collective-permute-start | bytes 98312 | tf_op jit(solution)/shard_map/ppermute | solution.py:17
  44.8 8.8 %collective-permute-start.5 = (bf16[32,512]{1,0:T(8,128)(2,1)S(1)}, bf16[32,512]{1,0:T(8,128)(2,1)S(1)}, u32[]{:S(2)}, u32[]{:S(2)}) collective-permute-start(bf16[32,512]{1,0:T(8,128)(2,1)S(1)} %select_select_fusion.6), channel_id=1, source_target_pairs={{4,0},{8,4},{12,8},{16,12},{20,16},{24,20},{28,24},{5,1},{9,5},{13... | collective-permute-start | bytes 98312 | tf_op jit(solution)/shard_map/ppermute | solution.py:17
  46.1 9.1 %collective-permute-start.6 = (bf16[32,512]{1,0:T(8,128)(2,1)S(1)}, bf16[32,512]{1,0:T(8,128)(2,1)S(1)}, u32[]{:S(2)}, u32[]{:S(2)}) collective-permute-start(bf16[32,512]{1,0:T(8,128)(2,1)S(1)} %select_select_fusion.5), channel_id=1, source_target_pairs={{0,8},{4,12},{8,16},{12,20},{16,24},{20,28},{1,9},{5,13},{9,17},{1... | collective-permute-start | bytes 98312 | tf_op jit(solution)/shard_map/ppermute | solution.py:17
  59.4 4.1 %copy-start.32 = (pred[32]{0:T(512)(128)(4,1)S(1)}, pred[32]{0:T(512)(128)(4,1)}, u32[]{:S(2)}) copy-start(pred[32]{0:T(512)(128)(4,1)} %copy-done.31) | copy-start | bytes 100
  59.4 4.2 %copy-start.28 = (pred[32]{0:T(512)(128)(4,1)S(1)}, pred[32]{0:T(512)(128)(4,1)}, u32[]{:S(2)}) copy-start(pred[32]{0:T(512)(128)(4,1)} %copy-done.27) | copy-start | bytes 100
  59.4 22.3 %copy-start.26 = (s32[1024]{0:T(1024)S(1)}, s32[1024]{0:T(1024)}, u32[]{:S(2)}) copy-start(s32[1024]{0:T(1024)} %copy-done.25) | copy-start | bytes 12292
  59.8 22.4 %copy-start.43 = (pred[2,3]{1,0:T(4,128)(4,1)S(1)}, pred[2,3]{1,0:T(4,128)(4,1)}, u32[]{:S(2)}) copy-start(pred[2,3]{1,0:T(4,128)(4,1)} %copy-done.41) | copy-start | bytes 22
  60.1 22.5 %copy-start.45 = (pred[2,3]{1,0:T(4,128)(4,1)S(1)}, pred[2,3]{1,0:T(4,128)(4,1)}, u32[]{:S(2)}) copy-start(pred[2,3]{1,0:T(4,128)(4,1)} %copy-done.44) | copy-start | bytes 22
  63.7 12.6 %collective-permute-start.8 = (bf16[32,256]{1,0:T(8,128)(2,1)S(1)}, bf16[32,256]{1,0:T(8,128)(2,1)S(1)}, u32[]{:S(2)}, u32[]{:S(2)}) collective-permute-start(bf16[32,256]{1,0:T(8,128)(2,1)S(1)} %select_select_fusion.11), channel_id=1, source_target_pairs={{0,4},{4,8},{8,12},{12,16},{16,20},{20,24},{24,28},{1,5},{5,9},{9,... | collective-permute-start | bytes 49160 | tf_op jit(solution)/shard_map/ppermute | solution.py:17
  66.8 9.5 %collective-permute-start.9 = (bf16[32,256]{1,0:T(8,128)(2,1)S(1)}, bf16[32,256]{1,0:T(8,128)(2,1)S(1)}, u32[]{:S(2)}, u32[]{:S(2)}) collective-permute-start(bf16[32,256]{1,0:T(8,128)(2,1)S(1)} %select_select_fusion.10), channel_id=1, source_target_pairs={{4,0},{8,4},{12,8},{16,12},{20,16},{24,20},{28,24},{5,1},{9,5},{13... | collective-permute-start | bytes 49160 | tf_op jit(solution)/shard_map/ppermute | solution.py:17
  68.1 8.3 %collective-permute-start.10 = (bf16[32,256]{1,0:T(8,128)(2,1)S(1)}, bf16[32,256]{1,0:T(8,128)(2,1)S(1)}, u32[]{:S(2)}, u32[]{:S(2)}) collective-permute-start(bf16[32,256]{1,0:T(8,128)(2,1)S(1)} %select_select_fusion.9), channel_id=1, source_target_pairs={{0,8},{4,12},{8,16},{12,20},{16,24},{20,28},{1,9},{5,13},{9,17},{1... | collective-permute-start | bytes 49160 | tf_op jit(solution)/shard_map/ppermute | solution.py:17
  75.0 5.9 %collective-permute-start.11 = (bf16[32,256]{1,0:T(8,128)(2,1)S(1)}, bf16[32,256]{1,0:T(8,128)(2,1)S(1)}, u32[]{:S(2)}, u32[]{:S(2)}) collective-permute-start(bf16[32,256]{1,0:T(8,128)(2,1)S(1)} %select_select_fusion.8), channel_id=1, source_target_pairs={{8,0},{12,4},{16,8},{20,12},{24,16},{28,20},{9,1},{13,5},{17,9},{2... | collective-permute-start | bytes 49160 | tf_op jit(solution)/shard_map/ppermute | solution.py:17
  86.5 12.4 %collective-permute-start.12 = (bf16[32,512]{1,0:T(8,128)(2,1)S(1)}, bf16[32,512]{1,0:T(8,128)(2,1)S(1)}, u32[]{:S(2)}, u32[]{:S(2)}) collective-permute-start(bf16[32,512]{1,0:T(8,128)(2,1)S(1)} %select_select_fusion.3), channel_id=1, source_target_pairs={{0,4},{4,8},{8,12},{12,16},{16,20},{20,24},{24,28},{1,5},{5,9},{9,... | collective-permute-start | bytes 98312 | tf_op jit(solution)/shard_map/ppermute | solution.py:17
  89.1 11.1 %collective-permute-start.15 = (bf16[32,512]{1,0:T(8,128)(2,1)S(1)}, bf16[32,512]{1,0:T(8,128)(2,1)S(1)}, u32[]{:S(2)}, u32[]{:S(2)}) collective-permute-start(bf16[32,512]{1,0:T(8,128)(2,1)S(1)} %select_select_fusion), channel_id=1, source_target_pairs={{8,0},{12,4},{16,8},{20,12},{24,16},{28,20},{9,1},{13,5},{17,9},{2... | collective-permute-start | bytes 98312 | tf_op jit(solution)/shard_map/ppermute | solution.py:17
  90.4 8.4 %collective-permute-start.13 = (bf16[32,512]{1,0:T(8,128)(2,1)S(1)}, bf16[32,512]{1,0:T(8,128)(2,1)S(1)}, u32[]{:S(2)}, u32[]{:S(2)}) collective-permute-start(bf16[32,512]{1,0:T(8,128)(2,1)S(1)} %select_select_fusion.2), channel_id=1, source_target_pairs={{4,0},{8,4},{12,8},{16,12},{20,16},{24,20},{28,24},{5,1},{9,5},{13... | collective-permute-start | bytes 98312 | tf_op jit(solution)/shard_map/ppermute | solution.py:17
  91.7 8.5 %collective-permute-start.14 = (bf16[32,512]{1,0:T(8,128)(2,1)S(1)}, bf16[32,512]{1,0:T(8,128)(2,1)S(1)}, u32[]{:S(2)}, u32[]{:S(2)}) collective-permute-start(bf16[32,512]{1,0:T(8,128)(2,1)S(1)} %select_select_fusion.1), channel_id=1, source_target_pairs={{0,8},{4,12},{8,16},{12,20},{16,24},{20,28},{1,9},{5,13},{9,17},{1... | collective-permute-start | bytes 98312 | tf_op jit(solution)/shard_map/ppermute | solution.py:17
  121.8 4.5 %slice-start = ((f32[3,128,256]{2,0,1:T(4,128)}), f32[2,128,256]{2,0,1:T(2,128)S(1)}, s32[]{:S(2)}) async-start(f32[3,128,256]{2,0,1:T(4,128)} %copy-done.4), calls=%async_computation.1 | async-start | bytes 524288 | tf_op jit(solution)/shard_map/slice | solution.py:68
  123.8 16.3 %copy-start.8 = (f32[256,2,128]{2,1,0:T(2,128)S(1)}, f32[256,2,128]{2,1,0:T(2,128)}, u32[]{:S(2)}) copy-start(f32[256,2,128]{2,1,0:T(2,128)} %get-tuple-element.14) | copy-start | bytes 786436
  123.8 16.3 %copy-start.9 = (f32[256,2,128]{2,1,0:T(2,128)S(1)}, f32[256,2,128]{2,1,0:T(2,128)}, u32[]{:S(2)}) copy-start(f32[256,2,128]{2,1,0:T(2,128)} %get-tuple-element.15) | copy-start | bytes 786436
  123.8 13.2 %collective-permute-start.16 = (bf16[32,512]{1,0:T(8,128)(2,1)S(1)}, bf16[32,512]{1,0:T(8,128)(2,1)S(1)}, u32[]{:S(2)}, u32[]{:S(2)}) collective-permute-start(bf16[32,512]{1,0:T(8,128)(2,1)S(1)} %get-tuple-element.64), channel_id=1, source_target_pairs={{4,0},{8,4},{12,8},{16,12},{20,16},{24,20},{28,24},{5,1},{9,5},{13... | collective-permute-start | bytes 98312 | tf_op jit(solution)/shard_map/ppermute | solution.py:17
  126.4 10.7 %collective-permute-start.19 = (bf16[32,512]{1,0:T(8,128)(2,1)S(1)}, bf16[32,512]{1,0:T(8,128)(2,1)S(1)}, u32[]{:S(2)}, u32[]{:S(2)}) collective-permute-start(bf16[32,512]{1,0:T(8,128)(2,1)S(1)} %get-tuple-element.65), channel_id=1, source_target_pairs={{0,8},{4,12},{8,16},{12,20},{16,24},{20,28},{1,9},{5,13},{9,17},{1... | collective-permute-start | bytes 98312 | tf_op jit(solution)/shard_map/ppermute | solution.py:17
  131.6 6.1 %collective-permute-start.18 = (bf16[32,512]{1,0:T(8,128)(2,1)S(1)}, bf16[32,512]{1,0:T(8,128)(2,1)S(1)}, u32[]{:S(2)}, u32[]{:S(2)}) collective-permute-start(bf16[32,512]{1,0:T(8,128)(2,1)S(1)} %get-tuple-element.66), channel_id=1, source_target_pairs={{8,0},{12,4},{16,8},{20,12},{24,16},{28,20},{9,1},{13,5},{17,9},{2... | collective-permute-start | bytes 98312 | tf_op jit(solution)/shard_map/ppermute | solution.py:17
  132.9 5.5 %collective-permute-start.17 = (bf16[32,512]{1,0:T(8,128)(2,1)S(1)}, bf16[32,512]{1,0:T(8,128)(2,1)S(1)}, u32[]{:S(2)}, u32[]{:S(2)}) collective-permute-start(bf16[32,512]{1,0:T(8,128)(2,1)S(1)} %get-tuple-element.67), channel_id=1, source_target_pairs={{0,4},{4,8},{8,12},{12,16},{16,20},{20,24},{24,28},{1,5},{5,9},{9,... | collective-permute-start | bytes 98312 | tf_op jit(solution)/shard_map/ppermute | solution.py:17
  142.9 14.0 %copy-start.6 = (f32[256,2,128]{2,1,0:T(2,128)S(1)}, f32[256,2,128]{2,1,0:T(2,128)}, u32[]{:S(2)}) copy-start(f32[256,2,128]{2,1,0:T(2,128)} %get-tuple-element.16) | copy-start | bytes 786436
  144.3 19.2 %copy-start.12 = (bf16[512,64]{0,1:T(8,128)(2,1)S(1)}, bf16[512,64]{0,1:T(8,128)(2,1)}, u32[]{:S(2)}) copy-start(bf16[512,64]{0,1:T(8,128)(2,1)} %copy-done.11) | copy-start | bytes 196612
  144.3 19.2 %copy-start.3 = (bf16[512,640]{1,0:T(8,128)(2,1)S(1)}, bf16[512,640]{1,0:T(8,128)(2,1)}, u32[]{:S(2)}) copy-start(bf16[512,640]{1,0:T(8,128)(2,1)} %copy-done.2) | copy-start | bytes 1966084
  144.3 19.2 %copy-start.10 = (bf16[512,64]{0,1:T(8,128)(2,1)S(1)}, bf16[512,64]{0,1:T(8,128)(2,1)}, u32[]{:S(2)}) copy-start(bf16[512,64]{0,1:T(8,128)(2,1)} %get-tuple-element.39) | copy-start | bytes 196612
  144.6 12.4 %collective-permute-start.21 = (bf16[32,256]{1,0:T(8,128)(2,1)S(1)}, bf16[32,256]{1,0:T(8,128)(2,1)S(1)}, u32[]{:S(2)}, u32[]{:S(2)}) collective-permute-start(bf16[32,256]{1,0:T(8,128)(2,1)S(1)} %bitcast.359), channel_id=1, source_target_pairs={{0,4},{4,8},{8,12},{12,16},{16,20},{20,24},{24,28},{1,5},{5,9},{9,... | collective-permute-start | bytes 49160 | tf_op jit(solution)/shard_map/ppermute | solution.py:17
  148.9 8.2 %collective-permute-start.22 = (bf16[32,256]{1,0:T(8,128)(2,1)S(1)}, bf16[32,256]{1,0:T(8,128)(2,1)S(1)}, u32[]{:S(2)}, u32[]{:S(2)}) collective-permute-start(bf16[32,256]{1,0:T(8,128)(2,1)S(1)} %bitcast.358), channel_id=1, source_target_pairs={{8,0},{12,4},{16,8},{20,12},{24,16},{28,20},{9,1},{13,5},{17,9},{2... | collective-permute-start | bytes 49160 | tf_op jit(solution)/shard_map/ppermute | solution.py:17
  150.2 6.9 %collective-permute-start.23 = (bf16[32,256]{1,0:T(8,128)(2,1)S(1)}, bf16[32,256]{1,0:T(8,128)(2,1)S(1)}, u32[]{:S(2)}, u32[]{:S(2)}) collective-permute-start(bf16[32,256]{1,0:T(8,128)(2,1)S(1)} %bitcast.356), channel_id=1, source_target_pairs={{0,8},{4,12},{8,16},{12,20},{16,24},{20,28},{1,9},{5,13},{9,17},{1... | collective-permute-start | bytes 49160 | tf_op jit(solution)/shard_map/ppermute | solution.py:17
  155.6 6.0 %collective-permute-start.20 = (bf16[32,256]{1,0:T(8,128)(2,1)S(1)}, bf16[32,256]{1,0:T(8,128)(2,1)S(1)}, u32[]{:S(2)}, u32[]{:S(2)}) collective-permute-start(bf16[32,256]{1,0:T(8,128)(2,1)S(1)} %bitcast.354), channel_id=1, source_target_pairs={{4,0},{8,4},{12,8},{16,12},{20,16},{24,20},{28,24},{5,1},{9,5},{13... | collective-permute-start | bytes 49160 | tf_op jit(solution)/shard_map/ppermute | solution.py:17
  156.9 8.4 %copy-start.20 = (bf16[640,128]{1,0:T(8,128)(2,1)S(1)}, bf16[640,128]{1,0:T(8,128)(2,1)}, u32[]{:S(2)}) copy-start(bf16[640,128]{1,0:T(8,128)(2,1)} %param.22) | copy-start | bytes 491524
  221.8 4.1 %copy-start.46 = (f32[64]{0:T(128)S(1)}, f32[64]{0:T(128)}, u32[]{:S(2)}) copy-start(f32[64]{0:T(128)} %get-tuple-element.20) | copy-start | bytes 772
  223.7 16.8 %copy-start.7 = (f32[256,2,128]{2,1,0:T(2,128)S(1)}, f32[256,2,128]{2,1,0:T(2,128)}, u32[]{:S(2)}) copy-start(f32[256,2,128]{2,1,0:T(2,128)} %get-tuple-element.9) | copy-start | bytes 786436
  224.6 11.0 %collective-permute-start.24 = (bf16[32,512]{1,0:T(8,128)(2,1)S(1)}, bf16[32,512]{1,0:T(8,128)(2,1)S(1)}, u32[]{:S(2)}, u32[]{:S(2)}) collective-permute-start(bf16[32,512]{1,0:T(8,128)(2,1)S(1)} %get-tuple-element.56), channel_id=1, source_target_pairs={{4,0},{8,4},{12,8},{16,12},{20,16},{24,20},{28,24},{5,1},{9,5},{13... | collective-permute-start | bytes 98312 | tf_op jit(solution)/shard_map/ppermute | solution.py:17
  226.7 9.0 %collective-permute-start.27 = (bf16[32,512]{1,0:T(8,128)(2,1)S(1)}, bf16[32,512]{1,0:T(8,128)(2,1)S(1)}, u32[]{:S(2)}, u32[]{:S(2)}) collective-permute-start(bf16[32,512]{1,0:T(8,128)(2,1)S(1)} %get-tuple-element.57), channel_id=1, source_target_pairs={{0,8},{4,12},{8,16},{12,20},{16,24},{20,28},{1,9},{5,13},{9,17},{1... | collective-permute-start | bytes 98312 | tf_op jit(solution)/shard_map/ppermute | solution.py:17
  232.9 5.8 %collective-permute-start.26 = (bf16[32,512]{1,0:T(8,128)(2,1)S(1)}, bf16[32,512]{1,0:T(8,128)(2,1)S(1)}, u32[]{:S(2)}, u32[]{:S(2)}) collective-permute-start(bf16[32,512]{1,0:T(8,128)(2,1)S(1)} %get-tuple-element.58), channel_id=1, source_target_pairs={{8,0},{12,4},{16,8},{20,12},{24,16},{28,20},{9,1},{13,5},{17,9},{2... | collective-permute-start | bytes 98312 | tf_op jit(solution)/shard_map/ppermute | solution.py:17
  234.2 4.6 %collective-permute-start.25 = (bf16[32,512]{1,0:T(8,128)(2,1)S(1)}, bf16[32,512]{1,0:T(8,128)(2,1)S(1)}, u32[]{:S(2)}, u32[]{:S(2)}) collective-permute-start(bf16[32,512]{1,0:T(8,128)(2,1)S(1)} %get-tuple-element.59), channel_id=1, source_target_pairs={{0,4},{4,8},{8,12},{12,16},{16,20},{20,24},{24,28},{1,5},{5,9},{9,... | collective-permute-start | bytes 98312 | tf_op jit(solution)/shard_map/ppermute | solution.py:17
  246.5 14.5 %copy-start.5 = (f32[256,2,128]{2,1,0:T(2,128)S(1)}, f32[256,2,128]{2,1,0:T(2,128)}, u32[]{:S(2)}) copy-start(f32[256,2,128]{2,1,0:T(2,128)} %get-tuple-element.11) | copy-start | bytes 786436
  248.8 12.1 %collective-permute-start.29 = (bf16[32,256]{1,0:T(8,128)(2,1)S(1)}, bf16[32,256]{1,0:T(8,128)(2,1)S(1)}, u32[]{:S(2)}, u32[]{:S(2)}) collective-permute-start(bf16[32,256]{1,0:T(8,128)(2,1)S(1)} %bitcast.360), channel_id=1, source_target_pairs={{0,4},{4,8},{8,12},{12,16},{16,20},{20,24},{24,28},{1,5},{5,9},{9,... | collective-permute-start | bytes 49160 | tf_op jit(solution)/shard_map/ppermute | solution.py:17
  253.8 7.3 %collective-permute-start.30 = (bf16[32,256]{1,0:T(8,128)(2,1)S(1)}, bf16[32,256]{1,0:T(8,128)(2,1)S(1)}, u32[]{:S(2)}, u32[]{:S(2)}) collective-permute-start(bf16[32,256]{1,0:T(8,128)(2,1)S(1)} %bitcast.357), channel_id=1, source_target_pairs={{8,0},{12,4},{16,8},{20,12},{24,16},{28,20},{9,1},{13,5},{17,9},{2... | collective-permute-start | bytes 49160 | tf_op jit(solution)/shard_map/ppermute | solution.py:17
  255.1 6.1 %collective-permute-start.31 = (bf16[32,256]{1,0:T(8,128)(2,1)S(1)}, bf16[32,256]{1,0:T(8,128)(2,1)S(1)}, u32[]{:S(2)}, u32[]{:S(2)}) collective-permute-start(bf16[32,256]{1,0:T(8,128)(2,1)S(1)} %bitcast.355), channel_id=1, source_target_pairs={{0,8},{4,12},{8,16},{12,20},{16,24},{20,28},{1,9},{5,13},{9,17},{1... | collective-permute-start | bytes 49160 | tf_op jit(solution)/shard_map/ppermute | solution.py:17
  259.6 6.8 %collective-permute-start.28 = (bf16[32,256]{1,0:T(8,128)(2,1)S(1)}, bf16[32,256]{1,0:T(8,128)(2,1)S(1)}, u32[]{:S(2)}, u32[]{:S(2)}) collective-permute-start(bf16[32,256]{1,0:T(8,128)(2,1)S(1)} %bitcast.353), channel_id=1, source_target_pairs={{4,0},{8,4},{12,8},{16,12},{20,16},{24,20},{28,24},{5,1},{9,5},{13... | collective-permute-start | bytes 49160 | tf_op jit(solution)/shard_map/ppermute | solution.py:17
  (17 other events, 35.3 us)
Sparse Core Ops, SparseCore 0:
  235.7 129.9 all-reduce.3
where the time goes:
time: 383 us; the launch traced here: 376 us
  waiting for transfers between devices  117 us (31%)
  starting transfers between devices  96.8 us (25%)
  local copies, waits for them, and re-layouts  44.2 us (12%)
  blocking collectives  42.8 us (11%)
  other arithmetic  31.5 us (8%)
  matrix products  27.2 us (7%)
  between operations  16.8 us (4%)
    ppermute x32, starting transfers between devices, passed_along(): lax.ppermute(value, axis, [(source, source + steps) for source in range(i...  96.8 us
    psum x1, waiting for transfers between devices, on_device(): lax.psum((gate_sums, gate_totals, candidate_sums, candidate_totals), ('gr...  95.6 us
    psum x1, blocking collectives, on_device(): lax.psum((gate_sums, gate_totals, candidate_sums, candidate_totals), ('gr...  42.8 us
    ppermute x32, waiting for transfers between devices, passed_along(): lax.ppermute(value, axis, [(source, source + steps) for source in range(i...  21.3 us
    dot_general x8, matrix products, gather_back(): jnp.einsum('itb,itcm->bcm', select, products, precision=lax.Precision.HIG...  12.4 us
    gather x16, local copies, waits for them, and re-layouts, outgoing(): jnp.take(values, send_rows[0, number], axis=0)  11 us
  transfers between devices with their start and end apart: 33, of which 10 were waited for; matrix products, arithmetic and copies ran while one was open for 7% of the time, Pallas kernels for 0%

commit v1 on v0

v1 whole, which is shorter than its diff:
```python
import functools
import math

import jax
import jax.numpy as jnp
from jax import lax
from jax.experimental import pallas as pl
from jax.experimental.pallas import tpu as pltpu
from jax.sharding import PartitionSpec as P

HID = 64
KS = 5
CH = 128
MESH = pl.DeviceIdType.MESH
F32 = jnp.float32
BF16 = jnp.bfloat16


def rim_offsets(set_count):
    return [(number // 2 + 1) * (1 - 2 * (number % 2)) for number in range(set_count)]


def chunk_rows(rows, parts):
    return -(-(-(-rows // parts)) // 8) * 8


def nn(a, b):
    return lax.dot_general(a, b, (((1,), (0,)), ((), ())), preferred_element_type=F32)


def nt(a, b):
    return lax.dot_general(a, b, (((1,), (1,)), ((), ())), preferred_element_type=F32)


def tn(a, b):
    return lax.dot_general(a, b, (((0,), (0,)), ((), ())), preferred_element_type=F32)


class Rim:
    def __init__(self, n, me, offsets, sign, refs):
        self.n, self.me, self.sign = n, me, sign
        self.offsets = offsets
        self.out, self.into, self.send_sem, self.recv_sem = refs
        self.slot = self.out.shape[0] // len(offsets)

    def copy(self, j, device):
        rows = pl.ds(j * self.slot, self.slot)
        return pltpu.make_async_remote_copy(
            src_ref=self.out.at[rows],
            dst_ref=self.into.at[rows],
            send_sem=self.send_sem.at[j],
            recv_sem=self.recv_sem.at[j],
            device_id={"graph": device},
            device_id_type=MESH,
        )

    def each(self, sign, act):
        for j, offset in enumerate(self.offsets):
            other = self.me + sign * offset
            pl.when((other >= 0) & (other < self.n))(functools.partial(act, j, other))

    def start(self, value):
        self.out[...] = value.astype(BF16)
        self.each(self.sign, lambda j, other: self.copy(j, other).start())

    def arrived(self):
        self.each(-self.sign, lambda j, other: self.copy(j, other).wait_recv())
        return self.into[...]

    def finish(self):
        self.each(self.sign, lambda j, other: self.copy(j, other).wait_send())


class Total:
    def __init__(self, nb, ng, mb, mg, refs):
        self.nb, self.ng, self.mb, self.mg = nb, ng, mb, mg
        self.stage, self.mine, self.got, self.part, self.heard, self.slab, self.out = refs[:7]
        self.sems = refs[7:]
        self.started = []

    def copy(self, phase, axis, count, me, src, dst):
        send_sem, recv_sem = self.sems[2 * phase], self.sems[2 * phase + 1]
        for d in range(1, count):
            other = lax.rem(me + d, count)
            c = pltpu.make_async_remote_copy(
                src_ref=src(other),
                dst_ref=dst(d),
                send_sem=send_sem.at[d],
                recv_sem=recv_sem.at[d],
                device_id={axis: other},
                device_id_type=MESH,
            )
            c.start()
            self.started.append(c)
        return self.started[len(self.started) - (count - 1) :] if count > 1 else []

    def phase1(self):
        self.mine[...] = self.stage[...].reshape(self.mine.shape).astype(BF16)
        self.wait = self.copy(
            0, "batch", self.nb, self.mb, lambda o: self.mine.at[o], lambda d: self.got.at[d]
        )

    def phase2(self):
        for c in self.wait:
            c.wait_recv()
        total = self.mine[self.mb].astype(F32)
        for d in range(1, self.nb):
            total += self.got[d].astype(F32)
        self.part[...] = total.reshape(self.part.shape).astype(BF16)
        self.wait = self.copy(
            1, "graph", self.ng, self.mg, lambda o: self.part.at[o], lambda d: self.heard.at[d]
        )

    def phase3(self):
        for c in self.wait:
            c.wait_recv()
        total = self.part[self.mg].astype(F32)
        for d in range(1, self.ng):
            total += self.heard[d].astype(F32)
        self.slab[self.mg] = total.astype(BF16)
        self.wait = self.copy(
            2,
            "graph",
            self.ng,
            self.mg,
            lambda o: self.slab.at[self.mg],
            lambda d: self.slab.at[self.mg],
        )

    def phase4(self):
        for c in self.wait:
            c.wait_recv()
        self.wait = self.copy(
            3, "batch", self.nb, self.mb, lambda o: self.slab, lambda d: self.out.at[self.mb]
        )
        self.out[self.mb] = self.slab[...]

    def phase5(self):
        for c in self.wait:
            c.wait_recv()

    def finish(self):
        for c in self.started:
            c.wait_send()


def step_kernel(
    ng,
    nb,
    counts,
    x_ref,
    h_ref,
    cot_ref,
    wg_ref,
    bias_ref,
    wc_ref,
    ft_ref,
    fc_ref,
    rt_ref,
    rc_ref,
    list_ref,
    list_row_ref,
    in_grad_ref,
    state_grad_ref,
    total1_ref,
    total2_ref,
    *scratch,
):
    set_count, slot = counts
    mg, mb = lax.axis_index("graph"), lax.axis_index("batch")
    nodes = x_ref.shape[0]
    w = x_ref.shape[1]
    half = w // 2
    tile = ft_ref.shape[2]
    rows_i, tpr = ft_ref.shape[:2]
    halo = set_count * slot
    blocks = (nodes + halo) // tile
    offsets = rim_offsets(set_count)
    wgx, wcx, a_ref, at_ref, sup_ref, cand_ref, g_ref = scratch[:7]
    rest = list(scratch[7:])
    signs = (1, 1, 1, 1, -1, -1, -1, -1)
    rims = [Rim(ng, mg, offsets, signs[e], rest[4 * e : 4 * e + 4]) for e in range(8)]
    rest = rest[32:]
    sum1 = Total(nb, ng, mb, mg, rest[:6] + [total1_ref] + rest[6:14])
    rest = rest[14:]
    sum2 = Total(nb, ng, mb, mg, rest[:6] + [total2_ref] + rest[6:14])

    for rim in rims:
        rim.into[...] = jnp.zeros(rim.into.shape, BF16)
    barrier = pltpu.get_barrier_semaphore()
    for d in range(1, ng):
        pl.semaphore_signal(
            barrier, inc=1, device_id={"graph": lax.rem(mg + d, ng)}, device_id_type=MESH
        )
    for d in range(1, nb):
        pl.semaphore_signal(
            barrier, inc=1, device_id={"batch": lax.rem(mb + d, nb)}, device_id_type=MESH
        )

    listed = list_ref[...]
    sel = jnp.where(
        lax.broadcasted_iota(jnp.int32, (halo, nodes), 1) == listed, 1.0, 0.0
    ).astype(BF16)
    sel_t = jnp.where(
        lax.broadcasted_iota(jnp.int32, (nodes, halo), 0) == list_row_ref[...], 1.0, 0.0
    ).astype(BF16)

    x = x_ref[...]
    h = h_ref[...]
    sup_ref[:, :w] = x
    sup_ref[:, w : 2 * w] = h
    values = sup_ref[:, : 2 * w]
    first = nn(sel, values)
    pl.semaphore_wait(barrier, ng + nb - 2)
    rims[0].start(first)

    for side, (tiles, cols) in enumerate(((ft_ref, fc_ref), (rt_ref, rc_ref))):
        for i in range(rows_i):
            for b in range(blocks):
                acc = None
                for t in range(tpr):
                    keep = (cols[i, t] == b).astype(F32)
                    term = tiles[i, t].astype(F32) * keep
                    acc = term if acc is None else acc + term
                r0 = side * nodes + i * tile
                a_ref[r0 : r0 + tile, b * tile : (b + 1) * tile] = acc.astype(BF16)
                at_ref[b * tile : (b + 1) * tile, r0 : r0 + tile] = acc.T.astype(BF16)

    own = a_ref[:, :nodes]
    local13 = nn(own, values)

    def widen(weight, columns, outs):
        pieces = []
        for k in range(KS):
            low = weight[k * CH : k * CH + half]
            high = weight[k * CH + half : (k + 1) * CH]
            pieces += [low, low, high, high]
        tall = jnp.concatenate(pieces, 0)
        i = lax.broadcasted_iota(jnp.int32, (columns, outs), 0)
        j = lax.broadcasted_iota(jnp.int32, (columns, outs), 1)
        pick = jnp.where(i == (j // w) * half + j % half, 1.0, 0.0).astype(BF16)
        wide = nn(tall, pick)
        i = lax.broadcasted_iota(jnp.int32, wide.shape, 0)
        j = lax.broadcasted_iota(jnp.int32, wide.shape, 1)
        return jnp.where((i // half) % 2 == (j // half) % 2, wide, 0.0).astype(BF16)

    wgx[...] = widen(wg_ref[...], 2 * HID, 2 * w)
    wcx[...] = widen(wc_ref[...], HID, w)

    s13 = local13 + nn(a_ref[:, nodes:], rims[0].arrived())
    s1 = s13[:nodes].astype(BF16)
    s3 = s13[nodes:].astype(BF16)
    sup_ref[:, 2 * w : 4 * w] = s1
    sup_ref[:, 6 * w : 8 * w] = s3
    rims[1].start(jnp.concatenate([nn(sel, s1), nn(sel, s3)], 1))
    base = values.astype(F32)
    l2 = nn(a_ref[:nodes, :nodes], s1)
    l4 = nn(a_ref[nodes:, :nodes], s3)
    pre = nn(values, wgx[: 2 * w]) + nn(s1, wgx[2 * w : 4 * w]) + nn(s3, wgx[6 * w : 8 * w])
    rim = rims[1].arrived()
    l2 += nn(a_ref[:nodes, nodes:], rim[:, : 2 * w])
    l4 += nn(a_ref[nodes:, nodes:], rim[:, 2 * w :])
    s2 = (2.0 * l2 - base).astype(BF16)
    s4 = (2.0 * l4 - base).astype(BF16)
    sup_ref[:, 4 * w : 6 * w] = s2
    sup_ref[:, 8 * w :] = s4
    pre += nn(s2, wgx[4 * w : 6 * w]) + nn(s4, wgx[8 * w :])
    hf = h.astype(F32)
    reset = jax.nn.sigmoid(pre[:, :w] + bias_ref[0:1, :])
    update = jax.nn.sigmoid(pre[:, w:] + bias_ref[1:2, :])

    gated = (reset * hf).astype(BF16)
    rims[2].start(nn(sel, gated))
    cand_ref[:, :w] = gated
    l13 = nn(own, gated)
    cpre = nn(gated, wcx[w : 2 * w])
    for k in range(KS):
        cpre += nn(sup_ref[:, 2 * k * w : (2 * k + 1) * w], wcx[2 * k * w : (2 * k + 1) * w])
    l13 += nn(a_ref[:, nodes:], rims[2].arrived())
    t1 = l13[:nodes].astype(BF16)
    t3 = l13[nodes:].astype(BF16)
    rims[3].start(jnp.concatenate([nn(sel, t1), nn(sel, t3)], 1))
    cand_ref[:, w : 2 * w] = t1
    cand_ref[:, 3 * w : 4 * w] = t3
    l2 = nn(a_ref[:nodes, :nodes], t1)
    l4 = nn(a_ref[nodes:, :nodes], t3)
    cpre += nn(t1, wcx[3 * w : 4 * w]) + nn(t3, wcx[7 * w : 8 * w])
    rim = rims[3].arrived()
    l2 += nn(a_ref[:nodes, nodes:], rim[:, :w])
    l4 += nn(a_ref[nodes:, nodes:], rim[:, w:])
    gatedf = gated.astype(F32)
    t2 = (2.0 * l2 - gatedf).astype(BF16)
    t4 = (2.0 * l4 - gatedf).astype(BF16)
    cand_ref[:, 2 * w : 3 * w] = t2
    cand_ref[:, 4 * w :] = t4
    cpre += nn(t2, wcx[5 * w : 6 * w]) + nn(t4, wcx[9 * w :])
    cand = jnp.tanh(cpre + bias_ref[2:3, :])

    cot = cot_ref[...].astype(F32)
    update_grad = cot * (hf - cand)
    cg = (cot * (1.0 - update) * (1.0 - cand * cand)).astype(BF16)
    gu = (update_grad * update * (1.0 - update)).astype(BF16)

    def cand_cot(k, part):
        r0 = (2 * k + part) * w
        return nt(cg, wcx[r0 : r0 + w])

    c2, c4 = cand_cot(2, 1), cand_cot(4, 1)
    c2b, c4b = c2.astype(BF16), c4.astype(BF16)
    atf, atr = at_ref[:, :nodes], at_ref[:, nodes:]
    rims[4].start(jnp.concatenate([nn(atf[nodes:], c2b), nn(atr[nodes:], c4b)], 1))
    f1 = cand_cot(1, 1) + 2.0 * nn(atf[:nodes], c2b)
    f3 = cand_cot(3, 1) + 2.0 * nn(atr[:nodes], c4b)
    rest_h = cand_cot(0, 1) - c2 - c4

    low = lax.broadcasted_iota(jnp.int32, (half, w), 1) < half

    def fold(m):
        t = jnp.where(low[:1] if m[0].shape[0] == 1 else low, m[0], m[1])
        return t + pltpu.roll(t, half, 1)

    def colsum(v):
        s = jnp.sum(v.astype(F32), 0, keepdims=True)
        s = jnp.broadcast_to(s, (8, w))
        return s + pltpu.roll(s, half, 1)

    def both(mx, mh):
        return [fold((mx[:half], mx[half:])), fold((mh[:half], mh[half:]))]

    low8 = low[:8]
    for k in range(KS):
        sx = sup_ref[:, 2 * k * w : (2 * k + 1) * w]
        sh = sup_ref[:, (2 * k + 1) * w : (2 * k + 2) * w]
        th = cand_ref[:, k * w : (k + 1) * w]
        yc = both(tn(sx, cg), tn(th, cg))
        yu = both(tn(sx, gu), tn(sh, gu))
        for part in range(2):
            r0 = k * CH + part * half
            sum1.stage[r0 : r0 + half] = jnp.where(low, yc[part], yu[part])
    used = KS * CH
    sum1.stage[used : used + 8] = jnp.where(low8, colsum(cg), colsum(gu))
    if sum1.stage.shape[0] > used + 8:
        sum1.stage[used + 8 :] = jnp.zeros((sum1.stage.shape[0] - used - 8, w), F32)
    sum1.phase1()

    back = nn(sel_t, rims[4].arrived())
    f1b = (f1 + 2.0 * back[:, :w]).astype(BF16)
    f3b = (f3 + 2.0 * back[:, w:]).astype(BF16)
    rims[5].start(nn(atf[nodes:], f1b) + nn(atr[nodes:], f3b))
    rest_h += nn(atf[:nodes], f1b) + nn(atr[:nodes], f3b)
    for k in range(KS):
        rows = slice(2 * k * w, 2 * (k + 1) * w)
        part = nt(gu, wgx[rows, w:])
        g_ref[:, 2 * k * w : (2 * k + 1) * w] = part[:, :w] + cand_cot(k, 0)
        g_ref[:, (2 * k + 1) * w : 2 * (k + 1) * w] = part[:, w:]
    sum1.phase2()
    gated_grad = rest_h + nn(sel_t, rims[5].arrived())

    gr = (gated_grad * hf * reset * (1.0 - reset)).astype(BF16)

    def gate_cot(k):
        cols = slice(2 * k * w, 2 * (k + 1) * w)
        return g_ref[:, cols] + nt(gr, wgx[cols, :w])

    g2, g4 = gate_cot(2), gate_cot(4)
    g2b, g4b = g2.astype(BF16), g4.astype(BF16)
    rims[6].start(jnp.concatenate([nn(atf[nodes:], g2b), nn(atr[nodes:], g4b)], 1))
    f1 = gate_cot(1) + 2.0 * nn(atf[:nodes], g2b)
    f3 = gate_cot(3) + 2.0 * nn(atr[:nodes], g4b)
    rest_all = gate_cot(0) - g2 - g4
    folded = []
    for k in range(KS):
        sx = sup_ref[:, 2 * k * w : (2 * k + 1) * w]
        sh = sup_ref[:, (2 * k + 1) * w : (2 * k + 2) * w]
        folded += both(tn(sx, gr), tn(sh, gr))
    for m in range(KS):
        sum2.stage[m * half : (m + 1) * half] = jnp.where(low, folded[m], folded[m + KS])
    used = KS * half
    sum2.stage[used : used + 8] = colsum(gr)
    if sum2.stage.shape[0] > used + 8:
        sum2.stage[used + 8 :] = jnp.zeros((sum2.stage.shape[0] - used - 8, w), F32)
    sum2.phase1()
    sum1.phase3()

    back = nn(sel_t, rims[6].arrived())
    f1b = (f1 + 2.0 * back[:, : 2 * w]).astype(BF16)
    f3b = (f3 + 2.0 * back[:, 2 * w :]).astype(BF16)
    rims[7].start(nn(atf[nodes:], f1b) + nn(atr[nodes:], f3b))
    rest_all += nn(atf[:nodes], f1b) + nn(atr[:nodes], f3b)
    sum2.phase2()
    sum1.phase4()
    rest_all += nn(sel_t, rims[7].arrived())
    sum2.phase3()
    in_grad_ref[...] = rest_all[:, :w]
    state_grad_ref[...] = cot * update + gated_grad * reset + rest_all[:, w:]
    sum2.phase4()
    sum1.phase5()
    sum2.phase5()
    for rim in rims:
        rim.finish()
    sum1.finish()
    sum2.finish()


def on_device(
    layer_input,
    hidden_state,
    hidden_grad,
    gate_weight,
    gate_bias,
    candidate_weight,
    candidate_bias,
    forward_tiles,
    forward_columns,
    reverse_tiles,
    reverse_columns,
    send_rows,
    send_count,
):
    ng, nb = lax.axis_size("graph"), lax.axis_size("batch")
    nodes, w = layer_input.shape
    set_count, slot = send_rows.shape[1:]
    halo = set_count * slot
    ids = jnp.arange(slot, dtype=jnp.int32)
    listed = jnp.where(ids[None, :] < send_count[0][:, None], send_rows[0], -1).reshape(halo, 1)
    reset_bias, update_bias = gate_bias[:HID], gate_bias[HID:]
    bias = jnp.stack(
        [jnp.concatenate([b, b]) for b in (reset_bias, update_bias, candidate_bias)]
    )
    r1 = chunk_rows(KS * CH + 8, ng * nb)
    r2 = chunk_rows(KS * CH // 2 + 8, ng * nb)
    widths = (2 * w, 4 * w, w, 2 * w, 2 * w, w, 4 * w, 2 * w)
    scratch = [
        pltpu.VMEM((KS * 2 * w, 2 * w), BF16),
        pltpu.VMEM((KS * 2 * w, w), BF16),
        pltpu.VMEM((2 * nodes, nodes + halo), BF16),
        pltpu.VMEM((nodes + halo, 2 * nodes), BF16),
        pltpu.VMEM((nodes, KS * 2 * w), BF16),
        pltpu.VMEM((nodes, KS * w), BF16),
        pltpu.VMEM((nodes, KS * 2 * w), F32),
    ]
    dma = lambda count: pltpu.SemaphoreType.DMA((count,))
    for width in widths:
        scratch += [
            pltpu.VMEM((halo, width), BF16),
            pltpu.VMEM((halo, width), BF16),
            dma(set_count),
            dma(set_count),
        ]
    for r in (r1, r2):
        scratch += [
            pltpu.VMEM((nb * ng * r, w), F32),
            pltpu.VMEM((nb, ng * r, w), BF16),
            pltpu.VMEM((nb, ng * r, w), BF16),
            pltpu.VMEM((ng, r, w), BF16),
            pltpu.VMEM((ng, r, w), BF16),
            pltpu.VMEM((ng, r, w), BF16),
            dma(nb),
            dma(nb),
            dma(ng),
            dma(ng),
            dma(ng),
            dma(ng),
            dma(nb),
            dma(nb),
        ]
    vmem = pl.BlockSpec(memory_space=pltpu.VMEM)
    smem = pl.BlockSpec(memory_space=pltpu.SMEM)
    input_grad, state_grad, total1, total2 = pl.pallas_call(
        functools.partial(step_kernel, ng, nb, (set_count, slot)),
        name="gru_backward",
        out_shape=(
            jax.ShapeDtypeStruct((nodes, w), F32),
            jax.ShapeDtypeStruct((nodes, w), F32),
            jax.ShapeDtypeStruct((nb, ng, r1, w), BF16),
            jax.ShapeDtypeStruct((nb, ng, r2, w), BF16),
        ),
        in_specs=[vmem] * 7 + [smem, vmem, smem, vmem, vmem],
        out_specs=(vmem,) * 4,
        scratch_shapes=scratch,
        compiler_params=pltpu.CompilerParams(
            collective_id=0, has_side_effects=True, vmem_limit_bytes=56 * 1024 * 1024
        ),
    )(
        layer_input,
        hidden_state,
        hidden_grad,
        gate_weight,
        bias,
        candidate_weight,
        forward_tiles,
        forward_columns,
        reverse_tiles,
        reverse_columns,
        listed,
        listed.reshape(1, halo),
    )
    samples = w // HID
    scale = 1.0 / math.sqrt(nodes * ng * samples * nb)
    total1 = total1.reshape(-1, w).astype(F32) * scale
    total2 = total2.reshape(-1, w).astype(F32) * scale
    used, used2 = KS * CH, KS * CH // 2
    reset_grads = jnp.concatenate([total2[:used2, :HID], total2[:used2, HID:]], 0)
    return (
        input_grad,
        state_grad,
        jnp.concatenate([reset_grads, total1[:used, HID:]], 1),
        jnp.concatenate([total2[used2, :HID], total1[used, HID:]]),
        total1[:used, :HID],
        total1[used, :HID],
    )


def solution(mesh):
    placed = (
        P("graph", "batch"),
        P("graph", "batch"),
        P("graph", "batch"),
        P(),
        P(),
        P(),
        P(),
        P("graph", None, None, None),
        P("graph", None),
        P("graph", None, None, None),
        P("graph", None),
        P("graph", None, None),
        P("graph", None),
    )
    return jax.shard_map(
        on_device,
        mesh=mesh,
        in_specs=placed,
        out_specs=(P("graph", "batch"), P("graph", "batch"), P(), P(), P(), P()),
        check_vma=False,
    )
```

time: 383 us -> 60.1 us (0.16); the launches traced: 376 us -> 59.8 us
  waiting for transfers between devices: 117 us -> 0 us
  starting transfers between devices: 96.8 us -> 0 us
  Pallas kernels: 0 us -> 47.8 us
  blocking collectives: 42.8 us -> 0 us
  local copies, waits for them, and re-layouts: 44.2 us -> 6.87 us
  matrix products: 27.2 us -> 0 us
  other arithmetic: 31.5 us -> 4.39 us
  between operations: 16.8 us -> 0.72 us
    ppermute x32 -> x0, starting transfers between devices: 96.8 us -> none  [passed_along(): lax.ppermute(value, axis, [(source, source + steps) for source in range(i...]
    psum x1 -> x0, waiting for transfers between devices: 95.6 us -> none  [on_device(): lax.psum((gate_sums, gate_totals, candidate_sums, candidate_totals), ('gr...]
    pallas_call x0 -> x1, Pallas kernels: none -> 47.8 us  [on_device(): pl.pallas_call(functools.partial(step_kernel, ng, nb, (set_count, slot)),...]
    psum x1 -> x0, blocking collectives: 42.8 us -> none  [on_device(): lax.psum((gate_sums, gate_totals, candidate_sums, candidate_totals), ('gr...]
    dot_general x30 -> x0, matrix products: 27.2 us -> none  [the longest x8 12.4 us: gather_back(): jnp.einsum('itb,itcm->bcm', select, products, precision=lax.Precision.HIG...]
    ppermute x32 -> x0, waiting for transfers between devices: 21.3 us -> none  [passed_along(): lax.ppermute(value, axis, [(source, source + steps) for source in range(i...]
    gather x28 -> x0, local copies, waits for them, and re-layouts: 16.9 us -> none  [the longest x16 11 us: outgoing(): jnp.take(values, send_rows[0, number], axis=0)]
    convert_element_type x15 -> x0, local copies, waits for them, and re-layouts: 7.69 us -> none  [the longest x4 5.87 us: back_supports(): members[2].astype(jnp.bfloat16)]
  transfers between devices with their start and end apart: 33 -> 0, of which waited for: 10 -> 0; matrix products, arithmetic and copies ran while one was open for 7% -> 0% of each run, Pallas kernels for 0% -> 0%
where the time goes in v1:
time: 60.1 us; the launch traced here: 59.8 us
  Pallas kernels  47.8 us (80%)
  local copies, waits for them, and re-layouts  6.87 us (11%)
  other arithmetic  4.39 us (7%)
  between operations  0.72 us (1%)
    pallas_call x1, Pallas kernels, on_device(): pl.pallas_call(functools.partial(step_kernel, ng, nb, (set_count, slot)),...  47.8 us
    unnamed x20, local copies, waits for them, and re-layouts  5.63 us

profile of v1, /device:TPU:0, one launch (start us, length us, event | category | flops | bytes accessed | tf_op | source)
XLA Modules:
  0.0 59.8 jit_solution(15430044952146771466)
XLA Ops:
  0.6 0.0 copy-start.6
  0.6 0.6 %copy-done.6 = s32[1,4]{1,0:T(1,128)S(1)} copy-done((s32[1,4]{1,0:T(1,128)S(1)}, s32[1,4]{1,0:T(1,128)}, u32[]{:S(2)}) %copy-start.6) | copy-done | bytes 40
  1.3 0.0 copy-start.7
  1.3 0.1 iota_compare_fusion
  1.4 0.0 copy-start.4
  1.4 0.1 lt.40
  1.5 0.5 copy-done.7
  1.9 0.1 maximum_bitcast_fusion.2
  2.0 0.0 copy-done.4
  2.0 0.1 squeeze.15
  2.1 0.0 copy-start.5
  2.1 0.5 broadcast_select_fusion.1.list_row_ref
  2.6 0.1 copy-done.5
  2.8 0.1 fusion.2
  2.9 0.1 maximum_bitcast_fusion
  2.9 0.6 pad_maximum_fusion.1.bias_ref
  3.5 0.1 lt.41
  3.7 0.1 squeeze.19
  3.8 0.0 copy-start.3
  3.8 0.6 %broadcast_select_fusion.list_ref = s32[128,1]{1,0:T(8,128)} fusion(pred[128,1]{1,0:T(8,128)(4,1)S(1)} %lt.41, s32[128,1]{1,0:T(8,128)S(1)} %squeeze.19), kind=kLoop, calls=%fused_computation.3 | loop fusion | flops 128 | bytes 1152 | tf_op jit(solution)/shard_map/jit(_where)/select_n | solution.py:425
  4.4 0.2 copy-done.3
  4.7 0.8 %copy.21.wc_ref = bf16[640,64]{1,0:T(8,128)(2,1)} copy(bf16[640,64]{0,1:T(8,128)(2,1)S(1)} %copy-done.3) | data formatting | bytes 163840 | tf_op args[5]
  5.5 47.8 %gru_backward.1 = (f32[256,128]{1,0:T(8,128)}, f32[256,128]{1,0:T(8,128)}, bf16[4,8,24,128]{3,2,1,0:T(8,128)(2,1)}, bf16[4,8,16,128]{3,2,1,0:T(8,128)(2,1)}) custom-call(bf16[256,128]{1,0:T(8,128)(2,1)} %x_ref.1, bf16[256,128]{1,0:T(8,128)(2,1)} %h_ref.1, bf16[256,128]{1,0:T(8,128)(2,1)} %cot_ref.1, bf16[640,128]{1,0:T(8,128)(2,1)} %wg_ref.1, ...), custom_call_target="tpu_custom_call" | custom-call | tf_op jit(solution)/shard_map/gru_backward/pallas_call | solution.py:469
  53.3 0.9 %convert_multiply_fusion.1 = f32[4,8,16,128]{3,2,1,0:T(8,128)S(1)} fusion(bf16[4,8,16,128]{3,2,1,0:T(8,128)(2,1)} %get-tuple-element.12), kind=kLoop, calls=%fused_computation.2 | loop fusion | flops 131072 | bytes 393216 | tf_op jit(solution)/shard_map/mul | solution.py:501
  54.2 0.0 copy-start
  54.2 0.1 fusion.1
  54.3 0.8 %copy-done = bf16[4,8,24,128]{3,2,1,0:T(8,128)(2,1)S(1)} copy-done((bf16[4,8,24,128]{3,2,1,0:T(8,128)(2,1)S(1)}, bf16[4,8,24,128]{3,2,1,0:T(8,128)(2,1)}, u32[]{:S(2)}) %copy-start) | copy-done | bytes 196632
  55.2 0.5 slice_bitcast_fusion
  55.7 0.6 pad_maximum_fusion.2
  56.3 0.2 fusion
  56.4 0.8 %copy.23 = f32[640,64]{0,1:T(8,128)} copy(f32[640,64]{1,0:T(8,128)S(1)} %get-tuple-element.16) | data formatting | bytes 327680
  57.3 0.0 copy-start.2
  57.3 0.9 %pad_maximum_fusion = f32[640,128]{1,0:T(8,128)} fusion(f32[640,64]{1,0:T(8,128)S(1)} %get-tuple-element.17, f32[320,64]{1,0:T(8,128)S(1)} %get-tuple-element.19, f32[320,64]{1,0:T(8,128)S(1)} %get-tuple-element.18), kind=kLoop, calls=%fused_computation.1 | loop fusion | flops 163840 | bytes 655360 | tf_op jit(solution)/shard_map/concatenate | solution.py:507
  58.1 0.0 copy-done.2
  58.2 0.0 copy-start.1
  58.2 0.7 %copy.26 = f32[256,128]{1,0:T(8,128)} copy(f32[256,128]{1,0:T(8,128)S(1)} %copy-done.2) | data formatting | bytes 262144
  58.8 0.3 copy-done.1
  59.1 0.7 %copy.27 = f32[256,128]{1,0:T(8,128)} copy(f32[256,128]{1,0:T(8,128)S(1)} %copy-done.1) | data formatting | bytes 262144
  (2 shorter events, 0.0 us)
Async XLA Ops:
  0.6 0.7 %copy-start.6 = (s32[1,4]{1,0:T(1,128)S(1)}, s32[1,4]{1,0:T(1,128)}, u32[]{:S(2)}) copy-start(s32[1,4]{1,0:T(1,128)} %param.25) | copy-start | bytes 52
  1.3 0.7 %copy-start.7 = (f32[64]{0:T(128)S(1)}, f32[64]{0:T(128)}, u32[]{:S(2)}) copy-start(f32[64]{0:T(128)} %param.19) | copy-start | bytes 772
  1.4 0.7 %copy-start.4 = (s32[1,4,32]{2,1,0:T(4,128)S(1)}, s32[1,4,32]{2,1,0:T(4,128)}, u32[]{:S(2)}) copy-start(s32[1,4,32]{2,1,0:T(4,128)} %param.24) | copy-start | bytes 1540
  2.1 0.7 %copy-start.5 = (f32[128]{0:T(128)S(1)}, f32[128]{0:T(128)}, u32[]{:S(2)}) copy-start(f32[128]{0:T(128)} %param.17) | copy-start | bytes 1540
  3.8 0.9 %copy-start.3 = (bf16[640,64]{0,1:T(8,128)(2,1)S(1)}, bf16[640,64]{0,1:T(8,128)(2,1)}, u32[]{:S(2)}) copy-start(bf16[640,64]{0,1:T(8,128)(2,1)} %param.18) | copy-start | bytes 245764
  54.2 0.9 %copy-start = (bf16[4,8,24,128]{3,2,1,0:T(8,128)(2,1)S(1)}, bf16[4,8,24,128]{3,2,1,0:T(8,128)(2,1)}, u32[]{:S(2)}) copy-start(bf16[4,8,24,128]{3,2,1,0:T(8,128)(2,1)} %get-tuple-element.13) | copy-start | bytes 589828
  57.3 0.9 %copy-start.2 = (f32[256,128]{1,0:T(8,128)S(1)}, f32[256,128]{1,0:T(8,128)}, u32[]{:S(2)}) copy-start(f32[256,128]{1,0:T(8,128)} %get-tuple-element.30) | copy-start | bytes 393220
  58.2 1.0 %copy-start.1 = (f32[256,128]{1,0:T(8,128)S(1)}, f32[256,128]{1,0:T(8,128)}, u32[]{:S(2)}) copy-start(f32[256,128]{1,0:T(8,128)} %get-tuple-element.31) | copy-start | bytes 393220

commit v2 on v1

--- a/solution.py
+++ b/solution.py
@@ -144,29 +144,79 @@
             c.wait_send()
 
 
+class Direct:
+    def __init__(self, nb, ng, mb, mg, refs):
+        self.n, self.ng = nb * ng, ng
+        self.me = mb * ng + mg
+        self.stage, self.mine, self.got, self.out = refs[:4]
+        self.sems = refs[4:]
+        self.started = []
+
+    def copy(self, phase, src, dst):
+        send_sem, recv_sem = self.sems[2 * phase], self.sems[2 * phase + 1]
+        self.wait = []
+        for d in range(1, self.n):
+            other = lax.rem(self.me + d, self.n)
+            c = pltpu.make_async_remote_copy(
+                src_ref=src(other),
+                dst_ref=dst(d),
+                send_sem=send_sem.at[d],
+                recv_sem=recv_sem.at[d],
+                device_id={"graph": lax.rem(other, self.ng), "batch": lax.div(other, self.ng)},
+                device_id_type=MESH,
+            )
+            c.start()
+            self.wait.append(c)
+        self.started += self.wait
+
+    def phase1(self):
+        self.mine[...] = self.stage[...].reshape(self.mine.shape).astype(BF16)
+        self.copy(0, lambda o: self.mine.at[o], lambda d: self.got.at[d])
+
+    def phase2(self):
+        for c in self.wait:
+            c.wait_recv()
+        total = self.mine[self.me].astype(F32)
+        for d in range(1, self.n):
+            total += self.got[d].astype(F32)
+        self.out[self.me] = total.astype(BF16)
+        self.copy(1, lambda o: self.out.at[self.me], lambda d: self.out.at[self.me])
+
+    def phase3(self):
+        for c in self.wait:
+            c.wait_recv()
+
+    def finish(self):
+        for c in self.started:
+            c.wait_send()
+
+
 def step_kernel(
     ng,
     nb,
-    counts,
+    scale,
     x_ref,
     h_ref,
     cot_ref,
     wg_ref,
-    bias_ref,
+    gate_bias_ref,
     wc_ref,
+    cand_bias_ref,
     ft_ref,
     fc_ref,
     rt_ref,
     rc_ref,
     list_ref,
-    list_row_ref,
+    count_ref,
     in_grad_ref,
     state_grad_ref,
-    total1_ref,
-    total2_ref,
+    gate_grad_ref,
+    gate_bias_grad_ref,
+    cand_grad_ref,
+    cand_bias_grad_ref,
     *scratch,
 ):
-    set_count, slot = counts
+    set_count, slot = list_ref.shape[1:]
     mg, mb = lax.axis_index("graph"), lax.axis_index("batch")
     nodes = x_ref.shape[0]
     w = x_ref.shape[1]
@@ -181,29 +231,35 @@
     signs = (1, 1, 1, 1, -1, -1, -1, -1)
     rims = [Rim(ng, mg, offsets, signs[e], rest[4 * e : 4 * e + 4]) for e in range(8)]
     rest = rest[32:]
-    sum1 = Total(nb, ng, mb, mg, rest[:6] + [total1_ref] + rest[6:14])
-    rest = rest[14:]
-    sum2 = Total(nb, ng, mb, mg, rest[:6] + [total2_ref] + rest[6:14])
+    sum1 = Total(nb, ng, mb, mg, rest[:15])
+    sum2 = Direct(nb, ng, mb, mg, rest[15:])
 
     for rim in rims:
         rim.into[...] = jnp.zeros(rim.into.shape, BF16)
     barrier = pltpu.get_barrier_semaphore()
-    for d in range(1, ng):
+    n, me = nb * ng, mb * ng + mg
+    for d in range(1, n):
+        other = lax.rem(me + d, n)
         pl.semaphore_signal(
-            barrier, inc=1, device_id={"graph": lax.rem(mg + d, ng)}, device_id_type=MESH
+            barrier,
+            inc=1,
+            device_id={"graph": lax.rem(other, ng), "batch": lax.div(other, ng)},
+            device_id_type=MESH,
         )
-    for d in range(1, nb):
-        pl.semaphore_signal(
-            barrier, inc=1, device_id={"batch": lax.rem(mb + d, nb)}, device_id_type=MESH
-        )
-
-    listed = list_ref[...]
-    sel = jnp.where(
-        lax.broadcasted_iota(jnp.int32, (halo, nodes), 1) == listed, 1.0, 0.0
-    ).astype(BF16)
-    sel_t = jnp.where(
-        lax.broadcasted_iota(jnp.int32, (nodes, halo), 0) == list_row_ref[...], 1.0, 0.0
-    ).astype(BF16)
+
+    ids = lax.broadcasted_iota(jnp.int32, (1, slot), 1)
+    listed = jnp.concatenate(
+        [jnp.where(ids < count_ref[0, j], list_ref[0, j : j + 1, :], -1) for j in range(set_count)],
+        1,
+    )
+    sel_f = jnp.where(
+        lax.broadcasted_iota(jnp.int32, (nodes, halo), 0)
+        == jnp.broadcast_to(listed, (nodes, halo)),
+        1.0,
+        0.0,
+    )
+    sel_t = sel_f.astype(BF16)
+    sel = sel_f.T.astype(BF16)
 
     x = x_ref[...]
     h = h_ref[...]
@@ -211,8 +267,6 @@
     sup_ref[:, w : 2 * w] = h
     values = sup_ref[:, : 2 * w]
     first = nn(sel, values)
-    pl.semaphore_wait(barrier, ng + nb - 2)
-    rims[0].start(first)
 
     for side, (tiles, cols) in enumerate(((ft_ref, fc_ref), (rt_ref, rc_ref))):
         for i in range(rows_i):
@@ -226,7 +280,13 @@
                 a_ref[r0 : r0 + tile, b * tile : (b + 1) * tile] = acc.astype(BF16)
                 at_ref[b * tile : (b + 1) * tile, r0 : r0 + tile] = acc.T.astype(BF16)
 
+    pl.semaphore_wait(barrier, n - 1)
+    rims[0].start(first)
+
     own = a_ref[:, :nodes]
+    af_sent = nn(sel, a_ref[:nodes, :]).astype(BF16)
+    ar_sent = nn(sel, a_ref[nodes:, :]).astype(BF16)
+    sent13 = [nn(m[:, :nodes], values) for m in (af_sent, ar_sent)]
     local13 = nn(own, values)
 
     def widen(weight, columns, outs):
@@ -245,14 +305,26 @@
         return jnp.where((i // half) % 2 == (j // half) % 2, wide, 0.0).astype(BF16)
 
     wgx[...] = widen(wg_ref[...], 2 * HID, 2 * w)
-    wcx[...] = widen(wc_ref[...], HID, w)
-
-    s13 = local13 + nn(a_ref[:, nodes:], rims[0].arrived())
+    wcx[...] = widen(wc_ref[...].astype(F32).T.astype(BF16), HID, w)
+    atf, atr = at_ref[:, :nodes], at_ref[:, nodes:]
+    af_back = nn(atf[nodes:], sel_t).astype(BF16)
+    ar_back = nn(atr[nodes:], sel_t).astype(BF16)
+
+    gate_bias = jnp.broadcast_to(gate_bias_ref[...], (8, w))
+    turned = pltpu.roll(gate_bias, half, 1)
+    low8 = lax.broadcasted_iota(jnp.int32, (8, w), 1) < half
+    reset_bias = jnp.where(low8, gate_bias, turned)[:1]
+    update_bias = jnp.where(low8, turned, gate_bias)[:1]
+    cand_bias = jnp.concatenate([cand_bias_ref[...]] * 2, 1)
+
+    rim = rims[0].arrived()
+    sent = [m + nn(a[:, nodes:], rim) for m, a in zip(sent13, (af_sent, ar_sent))]
+    rims[1].start(jnp.concatenate(sent, 1))
+    s13 = local13 + nn(a_ref[:, nodes:], rim)
     s1 = s13[:nodes].astype(BF16)
     s3 = s13[nodes:].astype(BF16)
     sup_ref[:, 2 * w : 4 * w] = s1
     sup_ref[:, 6 * w : 8 * w] = s3
-    rims[1].start(jnp.concatenate([nn(sel, s1), nn(sel, s3)], 1))
     base = values.astype(F32)
     l2 = nn(a_ref[:nodes, :nodes], s1)
     l4 = nn(a_ref[nodes:, :nodes], s3)
@@ -266,20 +338,23 @@
     sup_ref[:, 8 * w :] = s4
     pre += nn(s2, wgx[4 * w : 6 * w]) + nn(s4, wgx[8 * w :])
     hf = h.astype(F32)
-    reset = jax.nn.sigmoid(pre[:, :w] + bias_ref[0:1, :])
-    update = jax.nn.sigmoid(pre[:, w:] + bias_ref[1:2, :])
+    reset = jax.nn.sigmoid(pre[:, :w] + reset_bias)
+    update = jax.nn.sigmoid(pre[:, w:] + update_bias)
 
     gated = (reset * hf).astype(BF16)
     rims[2].start(nn(sel, gated))
     cand_ref[:, :w] = gated
+    sent13 = [nn(m[:, :nodes], gated) for m in (af_sent, ar_sent)]
     l13 = nn(own, gated)
     cpre = nn(gated, wcx[w : 2 * w])
     for k in range(KS):
         cpre += nn(sup_ref[:, 2 * k * w : (2 * k + 1) * w], wcx[2 * k * w : (2 * k + 1) * w])
-    l13 += nn(a_ref[:, nodes:], rims[2].arrived())
+    rim = rims[2].arrived()
+    sent = [m + nn(a[:, nodes:], rim) for m, a in zip(sent13, (af_sent, ar_sent))]
+    rims[3].start(jnp.concatenate(sent, 1))
+    l13 += nn(a_ref[:, nodes:], rim)
     t1 = l13[:nodes].astype(BF16)
     t3 = l13[nodes:].astype(BF16)
-    rims[3].start(jnp.concatenate([nn(sel, t1), nn(sel, t3)], 1))
     cand_ref[:, w : 2 * w] = t1
     cand_ref[:, 3 * w : 4 * w] = t3
     l2 = nn(a_ref[:nodes, :nodes], t1)
@@ -294,7 +369,7 @@
     cand_ref[:, 2 * w : 3 * w] = t2
     cand_ref[:, 4 * w :] = t4
     cpre += nn(t2, wcx[5 * w : 6 * w]) + nn(t4, wcx[9 * w :])
-    cand = jnp.tanh(cpre + bias_ref[2:3, :])
+    cand = jnp.tanh(cpre + cand_bias)
 
     cot = cot_ref[...].astype(F32)
     update_grad = cot * (hf - cand)
@@ -307,11 +382,13 @@
 
     c2, c4 = cand_cot(2, 1), cand_cot(4, 1)
     c2b, c4b = c2.astype(BF16), c4.astype(BF16)
-    atf, atr = at_ref[:, :nodes], at_ref[:, nodes:]
     rims[4].start(jnp.concatenate([nn(atf[nodes:], c2b), nn(atr[nodes:], c4b)], 1))
     f1 = cand_cot(1, 1) + 2.0 * nn(atf[:nodes], c2b)
     f3 = cand_cot(3, 1) + 2.0 * nn(atr[:nodes], c4b)
     rest_h = cand_cot(0, 1) - c2 - c4
+    f1b, f3b = f1.astype(BF16), f3.astype(BF16)
+    sent = nn(atf[nodes:], f1b) + nn(atr[nodes:], f3b)
+    rest_h += nn(atf[:nodes], f1b) + nn(atr[:nodes], f3b)
 
     low = lax.broadcasted_iota(jnp.int32, (half, w), 1) < half
 
@@ -327,7 +404,6 @@
     def both(mx, mh):
         return [fold((mx[:half], mx[half:])), fold((mh[:half], mh[half:]))]
 
-    low8 = low[:8]
     for k in range(KS):
         sx = sup_ref[:, 2 * k * w : (2 * k + 1) * w]
         sh = sup_ref[:, (2 * k + 1) * w : (2 * k + 2) * w]
@@ -343,11 +419,11 @@
         sum1.stage[used + 8 :] = jnp.zeros((sum1.stage.shape[0] - used - 8, w), F32)
     sum1.phase1()
 
-    back = nn(sel_t, rims[4].arrived())
-    f1b = (f1 + 2.0 * back[:, :w]).astype(BF16)
-    f3b = (f3 + 2.0 * back[:, w:]).astype(BF16)
-    rims[5].start(nn(atf[nodes:], f1b) + nn(atr[nodes:], f3b))
-    rest_h += nn(atf[:nodes], f1b) + nn(atr[:nodes], f3b)
+    rim = rims[4].arrived()
+    sent += 2.0 * (nn(af_back, rim[:, :w]) + nn(ar_back, rim[:, w:]))
+    rims[5].start(sent)
+    back = (2.0 * nn(sel_t, rim)).astype(BF16)
+    rest_h += nn(atf[:nodes], back[:, :w]) + nn(atr[:nodes], back[:, w:])
     for k in range(KS):
         rows = slice(2 * k * w, 2 * (k + 1) * w)
         part = nt(gu, wgx[rows, w:])
@@ -368,6 +444,8 @@
     f1 = gate_cot(1) + 2.0 * nn(atf[:nodes], g2b)
     f3 = gate_cot(3) + 2.0 * nn(atr[:nodes], g4b)
     rest_all = gate_cot(0) - g2 - g4
+    f1b, f3b = f1.astype(BF16), f3.astype(BF16)
+    sent = nn(atf[nodes:], f1b) + nn(atr[nodes:], f3b)
     folded = []
     for k in range(KS):
         sx = sup_ref[:, 2 * k * w : (2 * k + 1) * w]
@@ -382,20 +460,29 @@
     sum2.phase1()
     sum1.phase3()
 
-    back = nn(sel_t, rims[6].arrived())
-    f1b = (f1 + 2.0 * back[:, : 2 * w]).astype(BF16)
-    f3b = (f3 + 2.0 * back[:, 2 * w :]).astype(BF16)
-    rims[7].start(nn(atf[nodes:], f1b) + nn(atr[nodes:], f3b))
+    rim = rims[6].arrived()
+    sent += 2.0 * (nn(af_back, rim[:, : 2 * w]) + nn(ar_back, rim[:, 2 * w :]))
+    rims[7].start(sent)
+    sum1.phase4()
+    back = (2.0 * nn(sel_t, rim)).astype(BF16)
     rest_all += nn(atf[:nodes], f1b) + nn(atr[:nodes], f3b)
+    rest_all += nn(atf[:nodes], back[:, : 2 * w]) + nn(atr[:nodes], back[:, 2 * w :])
     sum2.phase2()
-    sum1.phase4()
+    sum1.phase5()
+    used = KS * CH
+    total1 = sum1.out[...].reshape(-1, w)[: used + 8].astype(F32) * scale
+    cand_grad_ref[...] = total1[:used].T[:half]
+    cand_bias_grad_ref[...] = total1[used : used + 1, :half]
     rest_all += nn(sel_t, rims[7].arrived())
-    sum2.phase3()
     in_grad_ref[...] = rest_all[:, :w]
     state_grad_ref[...] = cot * update + gated_grad * reset + rest_all[:, w:]
-    sum2.phase4()
-    sum1.phase5()
-    sum2.phase5()
+    sum2.phase3()
+    used2 = used // 2
+    total2 = sum2.out[...].reshape(-1, w)[: used2 + 8].astype(F32) * scale
+    gate_bias_grad_ref[...] = jnp.where(low8, total2[used2:], total1[used:])[:1]
+    wide = jnp.broadcast_to(low[:1], (used2, w))
+    gate_grad_ref[:used2] = jnp.where(wide, total2[:used2], total1[:used2])
+    gate_grad_ref[used2:] = jnp.where(wide, pltpu.roll(total2[:used2], half, 1), total1[used2:used])
     for rim in rims:
         rim.finish()
     sum1.finish()
@@ -421,12 +508,6 @@
     nodes, w = layer_input.shape
     set_count, slot = send_rows.shape[1:]
     halo = set_count * slot
-    ids = jnp.arange(slot, dtype=jnp.int32)
-    listed = jnp.where(ids[None, :] < send_count[0][:, None], send_rows[0], -1).reshape(halo, 1)
-    reset_bias, update_bias = gate_bias[:HID], gate_bias[HID:]
-    bias = jnp.stack(
-        [jnp.concatenate([b, b]) for b in (reset_bias, update_bias, candidate_bias)]
-    )
     r1 = chunk_rows(KS * CH + 8, ng * nb)
     r2 = chunk_rows(KS * CH // 2 + 8, ng * nb)
     widths = (2 * w, 4 * w, w, 2 * w, 2 * w, w, 4 * w, 2 * w)
@@ -447,67 +528,67 @@
             dma(set_count),
             dma(set_count),
         ]
-    for r in (r1, r2):
-        scratch += [
-            pltpu.VMEM((nb * ng * r, w), F32),
-            pltpu.VMEM((nb, ng * r, w), BF16),
-            pltpu.VMEM((nb, ng * r, w), BF16),
-            pltpu.VMEM((ng, r, w), BF16),
-            pltpu.VMEM((ng, r, w), BF16),
-            pltpu.VMEM((ng, r, w), BF16),
-            dma(nb),
-            dma(nb),
-            dma(ng),
-            dma(ng),
-            dma(ng),
-            dma(ng),
-            dma(nb),
-            dma(nb),
-        ]
+    n = nb * ng
+    scratch += [
+        pltpu.VMEM((n * r1, w), F32),
+        pltpu.VMEM((nb, ng * r1, w), BF16),
+        pltpu.VMEM((nb, ng * r1, w), BF16),
+        pltpu.VMEM((ng, r1, w), BF16),
+        pltpu.VMEM((ng, r1, w), BF16),
+        pltpu.VMEM((ng, r1, w), BF16),
+        pltpu.VMEM((nb, ng, r1, w), BF16),
+    ]
+    scratch += [dma(count) for count in (nb, nb, ng, ng, ng, ng, nb, nb)]
+    scratch += [
+        pltpu.VMEM((n * r2, w), F32),
+        pltpu.VMEM((n, r2, w), BF16),
+        pltpu.VMEM((n, r2, w), BF16),
+        pltpu.VMEM((n, r2, w), BF16),
+    ]
+    scratch += [dma(n)] * 4
     vmem = pl.BlockSpec(memory_space=pltpu.VMEM)
     smem = pl.BlockSpec(memory_space=pltpu.SMEM)
-    input_grad, state_grad, total1, total2 = pl.pallas_call(
-        functools.partial(step_kernel, ng, nb, (set_count, slot)),
+    scale = 1.0 / math.sqrt(nodes * ng * (w // HID) * nb)
+    grads = pl.pallas_call(
+        functools.partial(step_kernel, ng, nb, scale),
         name="gru_backward",
         out_shape=(
             jax.ShapeDtypeStruct((nodes, w), F32),
             jax.ShapeDtypeStruct((nodes, w), F32),
-            jax.ShapeDtypeStruct((nb, ng, r1, w), BF16),
-            jax.ShapeDtypeStruct((nb, ng, r2, w), BF16),
+            jax.ShapeDtypeStruct((KS * CH, 2 * HID), F32),
+            jax.ShapeDtypeStruct((1, 2 * HID), F32),
+            jax.ShapeDtypeStruct((HID, KS * CH), F32),
+            jax.ShapeDtypeStruct((1, HID), F32),
         ),
-        in_specs=[vmem] * 7 + [smem, vmem, smem, vmem, vmem],
-        out_specs=(vmem,) * 4,
+        in_specs=[vmem] * 8 + [smem, vmem, smem, vmem, smem],
+        out_specs=(vmem,) * 6,
         scratch_shapes=scratch,
         compiler_params=pltpu.CompilerParams(
-            collective_id=0, has_side_effects=True, vmem_limit_bytes=56 * 1024 * 1024
+            collective_id=0, has_side_effects=True, vmem_limit_bytes=32 * 1024 * 1024
         ),
     )(
         layer_input,
         hidden_state,
         hidden_grad,
         gate_weight,
-        bias,
-        candidate_weight,
+        gate_bias.reshape(1, 2 * HID),
+        candidate_weight.T,
+        candidate_bias.reshape(1, HID),
         forward_tiles,
         forward_columns,
         reverse_tiles,
         reverse_columns,
-        listed,
-        listed.reshape(1, halo),
+        send_rows,
+        send_count,
     )
-    samples = w // HID
-    scale = 1.0 / math.sqrt(nodes * ng * samples * nb)
-    total1 = total1.reshape(-1, w).astype(F32) * scale
-    total2 = total2.reshape(-1, w).astype(F32) * scale
-    used, used2 = KS * CH, KS * CH // 2
-    reset_grads = jnp.concatenate([total2[:used2, :HID], total2[:used2, HID:]], 0)
+    input_grad, state_grad, gate_grad, gate_bias_grad, cand_grad, cand_bias_grad = grads
     return (
         input_grad,
         state_grad,
-        jnp.concatenate([reset_grads, total1[:used, HID:]], 1),
-        jnp.concatenate([total2[used2, :HID], total1[used, HID:]]),
-        total1[:used, :HID],
-        total1[used, :HID],
+        gate_grad,
+        gate_bias_grad.reshape(2 * HID),
+        cand_grad.T,
+        cand_bias_grad.reshape(HID),
     )
 
 

time: 60.1 us -> 55.2 us (0.918)
  other arithmetic: 4.39 us -> 0 us
  Pallas kernels: 47.8 us -> 43.5 us
  local copies, waits for them, and re-layouts: 6.87 us -> 10.6 us
    unnamed x20 -> x32, local copies, waits for them, and re-layouts: 5.63 us -> 10.6 us
    pallas_call x1, Pallas kernels: 47.8 us -> 43.5 us  [on_device(): pl.pallas_call(functools.partial(step_kernel, ng, nb, scale), name='gru_b...]
    concatenate x2 -> x0, other arithmetic: 1.46 us -> none  [the longest x1 0.88 us: on_device(): jnp.concatenate([reset_grads, total1[:used, HID:]], 1)]
    select_n x2 -> x0, other arithmetic: 1.15 us -> none  [on_device(): jnp.where(ids[None, :] < send_count[0][:, None], send_rows[0], -1)]
    mul x2 -> x0, other arithmetic: 0.95 us -> none  [the longest x1 0.92 us: on_device(): total2 = total2.reshape(-1, w).astype(F32) * scale]
    another operation x3 -> x0, other arithmetic: 0.74 us -> none  [on_device(): jnp.stack([jnp.concatenate([b, b]) for b in (reset_bias, update_bias, can...]
    squeeze x4 -> x0, local copies, waits for them, and re-layouts: 0.7 us -> none  [the longest x1 0.51 us: on_device(): total1[used, :HID]]
where the time goes in v2:
time: 55.2 us; the launch traced here: 54.8 us
  Pallas kernels  43.5 us (79%)
  local copies, waits for them, and re-layouts  10.6 us (19%)
  between operations  0.71 us (1%)
    pallas_call x1, Pallas kernels, on_device(): pl.pallas_call(functools.partial(step_kernel, ng, nb, scale), name='gru_b...  43.5 us
    unnamed x32, local copies, waits for them, and re-layouts  10.6 us

profile of v2, /device:TPU:0, one launch (start us, length us, event | category | flops | bytes accessed | tf_op | source)
XLA Modules:
  0.0 54.8 jit_solution(12391782758402848430)
XLA Ops:
  0.6 0.0 copy-start.9
  0.6 0.0 copy-start.11
  0.7 0.0 copy-start.12
  0.7 0.0 copy-start.7
  0.7 0.0 copy-start.8
  0.7 0.0 copy-start.10
  0.7 0.6 %copy-done.9 = s32[2,3]{1,0:T(2,128)S(1)} copy-done((s32[2,3]{1,0:T(2,128)S(1)}, s32[2,3]{1,0:T(2,128)}, u32[]{:S(2)}) %copy-start.9) | copy-done | bytes 48
  1.3 0.0 copy-done.11
  1.3 0.0 copy-done.12
  1.3 0.0 copy-done.7
  1.4 0.0 copy-done.8
  1.4 0.0 copy-done.10
  1.4 0.0 copy-start
  1.4 0.9 %copy-done = bf16[2,3,128,128]{3,2,1,0:T(8,128)(2,1)S(1)} copy-done((bf16[2,3,128,128]{3,2,1,0:T(8,128)(2,1)S(1)}, bf16[2,3,128,128]{3,2,1,0:T(8,128)(2,1)}, u32[]{:S(2)}) %copy-start) | copy-done | bytes 196632
  2.3 0.0 copy-start.1
  2.3 0.9 %copy-done.1 = bf16[2,3,128,128]{3,2,1,0:T(8,128)(2,1)S(1)} copy-done((bf16[2,3,128,128]{3,2,1,0:T(8,128)(2,1)S(1)}, bf16[2,3,128,128]{3,2,1,0:T(8,128)(2,1)}, u32[]{:S(2)}) %copy-start.1) | copy-done | bytes 196632
  3.2 0.0 copy-start.2
  3.2 0.9 %copy-done.2 = bf16[640,128]{1,0:T(8,128)(2,1)S(1)} copy-done((bf16[640,128]{1,0:T(8,128)(2,1)S(1)}, bf16[640,128]{1,0:T(8,128)(2,1)}, u32[]{:S(2)}) %copy-start.2) | copy-done | bytes 163864
  4.2 0.0 copy-start.3
  4.2 0.9 %copy-done.3 = bf16[640,64]{0,1:T(8,128)(2,1)S(1)} copy-done((bf16[640,64]{0,1:T(8,128)(2,1)S(1)}, bf16[640,64]{0,1:T(8,128)(2,1)}, u32[]{:S(2)}) %copy-start.3) | copy-done | bytes 81944
  5.0 0.0 copy-start.4
  5.0 0.8 %copy-done.4 = bf16[256,128]{1,0:T(8,128)(2,1)S(1)} copy-done((bf16[256,128]{1,0:T(8,128)(2,1)S(1)}, bf16[256,128]{1,0:T(8,128)(2,1)}, u32[]{:S(2)}) %copy-start.4) | copy-done | bytes 65560
  5.9 0.0 copy-start.5
  5.9 0.8 %copy-done.5 = bf16[256,128]{1,0:T(8,128)(2,1)S(1)} copy-done((bf16[256,128]{1,0:T(8,128)(2,1)S(1)}, bf16[256,128]{1,0:T(8,128)(2,1)}, u32[]{:S(2)}) %copy-start.5) | copy-done | bytes 65560
  6.7 0.0 copy-start.6
  6.7 0.8 %copy-done.6 = bf16[256,128]{1,0:T(8,128)(2,1)S(1)} copy-done((bf16[256,128]{1,0:T(8,128)(2,1)S(1)}, bf16[256,128]{1,0:T(8,128)(2,1)}, u32[]{:S(2)}) %copy-start.6) | copy-done | bytes 65560
  7.6 43.5 %gru_backward.1 = (f32[256,128]{1,0:T(8,128)S(1)}, f32[256,128]{1,0:T(8,128)S(1)}, f32[640,128]{1,0:T(8,128)S(1)}, f32[1,128]{1,0:T(1,128)S(1)}, f32[64,640]{1,0:T(8,128)S(1)}, /*index=5*/f32[1,64]{1,0:T(1,128)S(1)}) custom-call(bf16[256,128]{1,0:T(8,128)(2,1)S(1)} %copy-done.4, bf16[256,128]{1,0:T(8,128)(2,1)S(1)} %copy-done.5, ...), custom_call_target="tpu_custom_call" | custom-call | tf_op jit(solution)/shard_map/gru_backward/pallas_call | solution.py:552
  51.1 0.7 %copy.25 = f32[256,128]{1,0:T(8,128)} copy(f32[256,128]{1,0:T(8,128)S(1)} %get-tuple-element.24) | data formatting | bytes 262144
  51.7 0.7 %copy.26 = f32[256,128]{1,0:T(8,128)} copy(f32[256,128]{1,0:T(8,128)S(1)} %get-tuple-element.25) | data formatting | bytes 262144
  52.4 0.7 %copy.27 = f32[640,128]{1,0:T(8,128)} copy(f32[640,128]{1,0:T(8,128)S(1)} %get-tuple-element.26) | data formatting | bytes 655360
  53.1 0.5 copy.28
  53.6 0.7 %copy.29 = f32[640,64]{0,1:T(8,128)} copy(f32[640,64]{0,1:T(8,128)S(1)} %bitcast.6) | data formatting | bytes 327680
  54.3 0.5 copy.30
Async XLA Ops:
  0.6 0.7 %copy-start.9 = (s32[2,3]{1,0:T(2,128)S(1)}, s32[2,3]{1,0:T(2,128)}, u32[]{:S(2)}) copy-start(s32[2,3]{1,0:T(2,128)} %rc_ref.1) | copy-start | bytes 76
  0.6 0.7 %copy-start.11 = (f32[64]{0:T(128)S(1)}, f32[64]{0:T(128)}, u32[]{:S(2)}) copy-start(f32[64]{0:T(128)} %param.19) | copy-start | bytes 772
  0.7 0.7 %copy-start.12 = (s32[1,4]{1,0:T(1,128)S(1)}, s32[1,4]{1,0:T(1,128)}, u32[]{:S(2)}) copy-start(s32[1,4]{1,0:T(1,128)} %count_ref.1) | copy-start | bytes 52
  0.7 0.7 %copy-start.7 = (s32[1,4,32]{2,1,0:T(4,128)S(1)}, s32[1,4,32]{2,1,0:T(4,128)}, u32[]{:S(2)}) copy-start(s32[1,4,32]{2,1,0:T(4,128)} %list_ref.1) | copy-start | bytes 1540
  0.7 0.7 %copy-start.8 = (s32[2,3]{1,0:T(2,128)S(1)}, s32[2,3]{1,0:T(2,128)}, u32[]{:S(2)}) copy-start(s32[2,3]{1,0:T(2,128)} %fc_ref.1) | copy-start | bytes 76
  0.7 0.7 %copy-start.10 = (f32[128]{0:T(128)S(1)}, f32[128]{0:T(128)}, u32[]{:S(2)}) copy-start(f32[128]{0:T(128)} %param.17) | copy-start | bytes 1540
  1.4 0.9 %copy-start = (bf16[2,3,128,128]{3,2,1,0:T(8,128)(2,1)S(1)}, bf16[2,3,128,128]{3,2,1,0:T(8,128)(2,1)}, u32[]{:S(2)}) copy-start(bf16[2,3,128,128]{3,2,1,0:T(8,128)(2,1)} %ft_ref.1) | copy-start | bytes 589828
  2.3 0.9 %copy-start.1 = (bf16[2,3,128,128]{3,2,1,0:T(8,128)(2,1)S(1)}, bf16[2,3,128,128]{3,2,1,0:T(8,128)(2,1)}, u32[]{:S(2)}) copy-start(bf16[2,3,128,128]{3,2,1,0:T(8,128)(2,1)} %rt_ref.1) | copy-start | bytes 589828
  3.2 0.9 %copy-start.2 = (bf16[640,128]{1,0:T(8,128)(2,1)S(1)}, bf16[640,128]{1,0:T(8,128)(2,1)}, u32[]{:S(2)}) copy-start(bf16[640,128]{1,0:T(8,128)(2,1)} %wg_ref.1) | copy-start | bytes 491524
  4.2 0.9 %copy-start.3 = (bf16[640,64]{0,1:T(8,128)(2,1)S(1)}, bf16[640,64]{0,1:T(8,128)(2,1)}, u32[]{:S(2)}) copy-start(bf16[640,64]{0,1:T(8,128)(2,1)} %param.18) | copy-start | bytes 245764
  5.0 0.8 %copy-start.4 = (bf16[256,128]{1,0:T(8,128)(2,1)S(1)}, bf16[256,128]{1,0:T(8,128)(2,1)}, u32[]{:S(2)}) copy-start(bf16[256,128]{1,0:T(8,128)(2,1)} %x_ref.1) | copy-start | bytes 196612
  5.9 0.8 %copy-start.5 = (bf16[256,128]{1,0:T(8,128)(2,1)S(1)}, bf16[256,128]{1,0:T(8,128)(2,1)}, u32[]{:S(2)}) copy-start(bf16[256,128]{1,0:T(8,128)(2,1)} %h_ref.1) | copy-start | bytes 196612
  6.7 0.8 %copy-start.6 = (bf16[256,128]{1,0:T(8,128)(2,1)S(1)}, bf16[256,128]{1,0:T(8,128)(2,1)}, u32[]{:S(2)}) copy-start(bf16[256,128]{1,0:T(8,128)(2,1)} %cot_ref.1) | copy-start | bytes 196612

commit v3 on v2

--- a/solution.py
+++ b/solution.py
@@ -195,16 +195,16 @@
     ng,
     nb,
     scale,
-    x_ref,
-    h_ref,
-    cot_ref,
-    wg_ref,
-    gate_bias_ref,
-    wc_ref,
-    cand_bias_ref,
-    ft_ref,
+    x_hbm,
+    h_hbm,
+    cot_hbm,
+    wg_hbm,
+    gate_bias_hbm,
+    wc_hbm,
+    cand_bias_hbm,
+    ft_hbm,
     fc_ref,
-    rt_ref,
+    rt_hbm,
     rc_ref,
     list_ref,
     count_ref,
@@ -217,6 +217,17 @@
     *scratch,
 ):
     set_count, slot = list_ref.shape[1:]
+    fetch_sem = scratch[-1]
+    sources = (x_hbm, h_hbm, ft_hbm, rt_hbm, wg_hbm, wc_hbm, gate_bias_hbm, cand_bias_hbm, cot_hbm)
+    held = scratch[-10:-1]
+    scratch = scratch[:-10]
+    fetches = [
+        pltpu.make_async_copy(source, target, fetch_sem.at[number])
+        for number, (source, target) in enumerate(zip(sources, held))
+    ]
+    for fetch in fetches:
+        fetch.start()
+    x_ref, h_ref, ft_ref, rt_ref, wg_ref, wc_ref, gate_bias_ref, cand_bias_ref, cot_ref = held
     mg, mb = lax.axis_index("graph"), lax.axis_index("batch")
     nodes = x_ref.shape[0]
     w = x_ref.shape[1]
@@ -261,6 +272,8 @@
     sel_t = sel_f.astype(BF16)
     sel = sel_f.T.astype(BF16)
 
+    for fetch in fetches[:2]:
+        fetch.wait()
     x = x_ref[...]
     h = h_ref[...]
     sup_ref[:, :w] = x
@@ -268,6 +281,8 @@
     values = sup_ref[:, : 2 * w]
     first = nn(sel, values)
 
+    for fetch in fetches[2:4]:
+        fetch.wait()
     for side, (tiles, cols) in enumerate(((ft_ref, fc_ref), (rt_ref, rc_ref))):
         for i in range(rows_i):
             for b in range(blocks):
@@ -288,6 +303,9 @@
     ar_sent = nn(sel, a_ref[nodes:, :]).astype(BF16)
     sent13 = [nn(m[:, :nodes], values) for m in (af_sent, ar_sent)]
     local13 = nn(own, values)
+
+    for fetch in fetches[4:]:
+        fetch.wait()
 
     def widen(weight, columns, outs):
         pieces = []
@@ -487,6 +505,40 @@
         rim.finish()
     sum1.finish()
     sum2.finish()
+
+
+def deliver_kernel(count, *refs):
+    sources, targets, held = refs[:count], refs[count : 2 * count], refs[2 * count : 3 * count]
+    in_sem, out_sem = refs[3 * count :]
+    loads = [
+        pltpu.make_async_copy(sources[i], held[i], in_sem.at[i]) for i in range(count)
+    ]
+    stores = [
+        pltpu.make_async_copy(held[i], targets[i], out_sem.at[i]) for i in range(count)
+    ]
+    for load in loads:
+        load.start()
+    for load, store in zip(loads, stores):
+        load.wait()
+        store.start()
+    for store in stores:
+        store.wait()
+
+
+def deliver(arrays):
+    count = len(arrays)
+    shapes = [(a.shape, a.dtype) for a in arrays]
+    hbm = pl.BlockSpec(memory_space=pltpu.HBM)
+    return pl.pallas_call(
+        functools.partial(deliver_kernel, count),
+        name="deliver",
+        out_shape=tuple(jax.ShapeDtypeStruct(*shape) for shape in shapes),
+        in_specs=[hbm] * count,
+        out_specs=(hbm,) * count,
+        scratch_shapes=[pltpu.VMEM(*shape) for shape in shapes]
+        + [pltpu.SemaphoreType.DMA((count,))] * 2,
+        compiler_params=pltpu.CompilerParams(vmem_limit_bytes=60 * 1024 * 1024),
+    )(*arrays)
 
 
 def on_device(
@@ -546,7 +598,20 @@
         pltpu.VMEM((n, r2, w), BF16),
     ]
     scratch += [dma(n)] * 4
+    fetched = (
+        layer_input,
+        hidden_state,
+        forward_tiles,
+        reverse_tiles,
+        gate_weight,
+        candidate_weight.T,
+        gate_bias.reshape(1, 2 * HID),
+        candidate_bias.reshape(1, HID),
+        hidden_grad,
+    )
+    scratch += [pltpu.VMEM(a.shape, a.dtype) for a in fetched] + [dma(len(fetched))]
     vmem = pl.BlockSpec(memory_space=pltpu.VMEM)
+    hbm = pl.BlockSpec(memory_space=pltpu.HBM)
     smem = pl.BlockSpec(memory_space=pltpu.SMEM)
     scale = 1.0 / math.sqrt(nodes * ng * (w // HID) * nb)
     grads = pl.pallas_call(
@@ -560,11 +625,11 @@
             jax.ShapeDtypeStruct((HID, KS * CH), F32),
             jax.ShapeDtypeStruct((1, HID), F32),
         ),
-        in_specs=[vmem] * 8 + [smem, vmem, smem, vmem, smem],
+        in_specs=[hbm] * 8 + [smem, hbm, smem, vmem, smem],
         out_specs=(vmem,) * 6,
         scratch_shapes=scratch,
         compiler_params=pltpu.CompilerParams(
-            collective_id=0, has_side_effects=True, vmem_limit_bytes=32 * 1024 * 1024
+            collective_id=0, has_side_effects=True, vmem_limit_bytes=60 * 1024 * 1024
         ),
     )(
         layer_input,
@@ -581,7 +646,7 @@
         send_rows,
         send_count,
     )
-    input_grad, state_grad, gate_grad, gate_bias_grad, cand_grad, cand_bias_grad = grads
+    input_grad, state_grad, gate_grad, gate_bias_grad, cand_grad, cand_bias_grad = deliver(grads)
     return (
         input_grad,
         state_grad,

time: 55.2 us -> 47.6 us (0.86)
  local copies, waits for them, and re-layouts: 10.6 us -> 0 us
  Pallas kernels: 43.5 us -> 46.7 us
    unnamed x32 -> x0, local copies, waits for them, and re-layouts: 10.6 us -> none
    pallas_call x0 -> x1, Pallas kernels: none -> 1.99 us  [deliver(): pl.pallas_call(functools.partial(deliver_kernel, count), name='deliver',...]
    pallas_call x1, Pallas kernels: 43.5 us -> 44.7 us  [on_device(): pl.pallas_call(functools.partial(step_kernel, ng, nb, scale), name='gru_b...]
where the time goes in v3:
time: 47.6 us; the launch traced here: 47.4 us
  Pallas kernels  46.7 us (98%)
  between operations  0.65 us (1%)
    pallas_call x1, Pallas kernels, on_device(): pl.pallas_call(functools.partial(step_kernel, ng, nb, scale), name='gru_b...  44.7 us
    pallas_call x1, Pallas kernels, deliver(): pl.pallas_call(functools.partial(deliver_kernel, count), name='deliver',...  1.99 us

profile of v3, /device:TPU:0, one launch (start us, length us, event | category | flops | bytes accessed | tf_op | source)
XLA Modules:
  0.0 47.4 jit_solution(14463127416558748564)
XLA Ops:
  0.6 44.7 %gru_backward.1 = (f32[256,128]{1,0:T(8,128)}, f32[256,128]{1,0:T(8,128)}, f32[640,128]{1,0:T(8,128)}, f32[1,128]{1,0:T(1,128)}, f32[64,640]{1,0:T(8,128)}, /*index=5*/f32[1,64]{1,0:T(1,128)}) custom-call(bf16[256,128]{1,0:T(8,128)(2,1)} %x_hbm.1, bf16[256,128]{1,0:T(8,128)(2,1)} %h_hbm.1, bf16[256,128]{1,0:T(8,128)(2,1)} %cot_hbm.1, ...), custom_call_target="tpu_custom_call" | custom-call | tf_op jit(solution)/shard_map/gru_backward/pallas_call | solution.py:617
  45.4 2.0 %deliver.1 = (f32[256,128]{1,0:T(8,128)}, f32[256,128]{1,0:T(8,128)}, f32[640,128]{1,0:T(8,128)}, f32[1,128]{1,0:T(1,128)}, f32[64,640]{1,0:T(8,128)}, /*index=5*/f32[1,64]{1,0:T(1,128)}) custom-call(f32[256,128]{1,0:T(8,128)} %get-tuple-element.18.refs_0_, f32[256,128]{1,0:T(8,128)} %get-tuple-element.19.refs_1_, f32[640,128]{1,0:T(8,128)} %get-tuple-element.20.refs_2_, ...), custom_call_target="tpu_custom_call" | custom-call | tf_op jit(solution)/shard_map/deliver/pallas_call | solution.py:532

commit v4 on v3

--- a/solution.py
+++ b/solution.py
@@ -69,79 +69,6 @@
 
     def finish(self):
         self.each(self.sign, lambda j, other: self.copy(j, other).wait_send())
-
-
-class Total:
-    def __init__(self, nb, ng, mb, mg, refs):
-        self.nb, self.ng, self.mb, self.mg = nb, ng, mb, mg
-        self.stage, self.mine, self.got, self.part, self.heard, self.slab, self.out = refs[:7]
-        self.sems = refs[7:]
-        self.started = []
-
-    def copy(self, phase, axis, count, me, src, dst):
-        send_sem, recv_sem = self.sems[2 * phase], self.sems[2 * phase + 1]
-        for d in range(1, count):
-            other = lax.rem(me + d, count)
-            c = pltpu.make_async_remote_copy(
-                src_ref=src(other),
-                dst_ref=dst(d),
-                send_sem=send_sem.at[d],
-                recv_sem=recv_sem.at[d],
-                device_id={axis: other},
-                device_id_type=MESH,
-            )
-            c.start()
-            self.started.append(c)
-        return self.started[len(self.started) - (count - 1) :] if count > 1 else []
-
-    def phase1(self):
-        self.mine[...] = self.stage[...].reshape(self.mine.shape).astype(BF16)
-        self.wait = self.copy(
-            0, "batch", self.nb, self.mb, lambda o: self.mine.at[o], lambda d: self.got.at[d]
-        )
-
-    def phase2(self):
-        for c in self.wait:
-            c.wait_recv()
-        total = self.mine[self.mb].astype(F32)
-        for d in range(1, self.nb):
-            total += self.got[d].astype(F32)
-        self.part[...] = total.reshape(self.part.shape).astype(BF16)
-        self.wait = self.copy(
-            1, "graph", self.ng, self.mg, lambda o: self.part.at[o], lambda d: self.heard.at[d]
-        )
-
-    def phase3(self):
-        for c in self.wait:
-            c.wait_recv()
-        total = self.part[self.mg].astype(F32)
-        for d in range(1, self.ng):
-            total += self.heard[d].astype(F32)
-        self.slab[self.mg] = total.astype(BF16)
-        self.wait = self.copy(
-            2,
-            "graph",
-            self.ng,
-            self.mg,
-            lambda o: self.slab.at[self.mg],
-            lambda d: self.slab.at[self.mg],
-        )
-
-    def phase4(self):
-        for c in self.wait:
-            c.wait_recv()
-        self.wait = self.copy(
-            3, "batch", self.nb, self.mb, lambda o: self.slab, lambda d: self.out.at[self.mb]
-        )
-        self.out[self.mb] = self.slab[...]
-
-    def phase5(self):
-        for c in self.wait:
-            c.wait_recv()
-
-    def finish(self):
-        for c in self.started:
-            c.wait_send()
 
 
 class Direct:
@@ -242,8 +169,8 @@
     signs = (1, 1, 1, 1, -1, -1, -1, -1)
     rims = [Rim(ng, mg, offsets, signs[e], rest[4 * e : 4 * e + 4]) for e in range(8)]
     rest = rest[32:]
-    sum1 = Total(nb, ng, mb, mg, rest[:15])
-    sum2 = Direct(nb, ng, mb, mg, rest[15:])
+    sum1 = Direct(nb, ng, mb, mg, rest[:8])
+    sum2 = Direct(nb, ng, mb, mg, rest[8:])
 
     for rim in rims:
         rim.into[...] = jnp.zeros(rim.into.shape, BF16)
@@ -447,7 +374,6 @@
         part = nt(gu, wgx[rows, w:])
         g_ref[:, 2 * k * w : (2 * k + 1) * w] = part[:, :w] + cand_cot(k, 0)
         g_ref[:, (2 * k + 1) * w : 2 * (k + 1) * w] = part[:, w:]
-    sum1.phase2()
     gated_grad = rest_h + nn(sel_t, rims[5].arrived())
 
     gr = (gated_grad * hf * reset * (1.0 - reset)).astype(BF16)
@@ -476,17 +402,16 @@
     if sum2.stage.shape[0] > used + 8:
         sum2.stage[used + 8 :] = jnp.zeros((sum2.stage.shape[0] - used - 8, w), F32)
     sum2.phase1()
-    sum1.phase3()
+    sum1.phase2()
 
     rim = rims[6].arrived()
     sent += 2.0 * (nn(af_back, rim[:, : 2 * w]) + nn(ar_back, rim[:, 2 * w :]))
     rims[7].start(sent)
-    sum1.phase4()
     back = (2.0 * nn(sel_t, rim)).astype(BF16)
     rest_all += nn(atf[:nodes], f1b) + nn(atr[:nodes], f3b)
     rest_all += nn(atf[:nodes], back[:, : 2 * w]) + nn(atr[:nodes], back[:, 2 * w :])
     sum2.phase2()
-    sum1.phase5()
+    sum1.phase3()
     used = KS * CH
     total1 = sum1.out[...].reshape(-1, w)[: used + 8].astype(F32) * scale
     cand_grad_ref[...] = total1[:used].T[:half]
@@ -581,23 +506,14 @@
             dma(set_count),
         ]
     n = nb * ng
-    scratch += [
-        pltpu.VMEM((n * r1, w), F32),
-        pltpu.VMEM((nb, ng * r1, w), BF16),
-        pltpu.VMEM((nb, ng * r1, w), BF16),
-        pltpu.VMEM((ng, r1, w), BF16),
-        pltpu.VMEM((ng, r1, w), BF16),
-        pltpu.VMEM((ng, r1, w), BF16),
-        pltpu.VMEM((nb, ng, r1, w), BF16),
-    ]
-    scratch += [dma(count) for count in (nb, nb, ng, ng, ng, ng, nb, nb)]
-    scratch += [
-        pltpu.VMEM((n * r2, w), F32),
-        pltpu.VMEM((n, r2, w), BF16),
-        pltpu.VMEM((n, r2, w), BF16),
-        pltpu.VMEM((n, r2, w), BF16),
-    ]
-    scratch += [dma(n)] * 4
+    for r in (r1, r2):
+        scratch += [
+            pltpu.VMEM((n * r, w), F32),
+            pltpu.VMEM((n, r, w), BF16),
+            pltpu.VMEM((n, r, w), BF16),
+            pltpu.VMEM((n, r, w), BF16),
+        ]
+        scratch += [dma(n)] * 4
     fetched = (
         layer_input,
         hidden_state,

time: 47.6 us -> 49 us (1.029)
  Pallas kernels: 46.7 us -> 48.1 us
    pallas_call x1, Pallas kernels: 44.7 us -> 46.1 us  [on_device(): pl.pallas_call(functools.partial(step_kernel, ng, nb, scale), name='gru_b...]
where the time goes in v4:
time: 49 us; the launch traced here: 48.8 us
  Pallas kernels  48.1 us (98%)
  between operations  0.65 us (1%)
    pallas_call x1, Pallas kernels, on_device(): pl.pallas_call(functools.partial(step_kernel, ng, nb, scale), name='gru_b...  46.1 us
    pallas_call x1, Pallas kernels, deliver(): pl.pallas_call(functools.partial(deliver_kernel, count), name='deliver',...  1.99 us

profile of v4, /device:TPU:0, one launch (start us, length us, event | category | flops | bytes accessed | tf_op | source)
XLA Modules:
  0.0 48.8 jit_solution(7071628371845156450)
XLA Ops:
  0.6 46.1 %gru_backward.1 = (f32[256,128]{1,0:T(8,128)}, f32[256,128]{1,0:T(8,128)}, f32[640,128]{1,0:T(8,128)}, f32[1,128]{1,0:T(1,128)}, f32[64,640]{1,0:T(8,128)}, /*index=5*/f32[1,64]{1,0:T(1,128)}) custom-call(bf16[256,128]{1,0:T(8,128)(2,1)} %x_hbm.1, bf16[256,128]{1,0:T(8,128)(2,1)} %h_hbm.1, bf16[256,128]{1,0:T(8,128)(2,1)} %cot_hbm.1, ...), custom_call_target="tpu_custom_call" | custom-call | tf_op jit(solution)/shard_map/gru_backward/pallas_call | solution.py:533
  46.8 2.0 %deliver.1 = (f32[256,128]{1,0:T(8,128)}, f32[256,128]{1,0:T(8,128)}, f32[640,128]{1,0:T(8,128)}, f32[1,128]{1,0:T(1,128)}, f32[64,640]{1,0:T(8,128)}, /*index=5*/f32[1,64]{1,0:T(1,128)}) custom-call(f32[256,128]{1,0:T(8,128)} %get-tuple-element.18.refs_0_, f32[256,128]{1,0:T(8,128)} %get-tuple-element.19.refs_1_, f32[640,128]{1,0:T(8,128)} %get-tuple-element.20.refs_2_, ...), custom_call_target="tpu_custom_call" | custom-call | tf_op jit(solution)/shard_map/deliver/pallas_call | solution.py:457
